TPU v7x, 32 devices: a whole 2x2x4 slice. The times are simulated.
32 devices in a mesh: groups: 2 (over x), rows: 16 (over z, y, core).
Axes of the slice: x: 2, y: 2, z: 4, core: 2. Of those that a mesh axis runs over, the one named last changes fastest.
Arguments:
- token_ids: int32 [1, 256], P(None, 'groups'), parts along dimension 1, may hold values from 0 to 32767
- parents: int32 [1, 8, 32], P(None, 'groups'), parts along dimension 1, may hold values from 0 to 31, as said below
- states: bfloat16 [256, 16, 128, 128], P(('groups', 'rows')), parts along dimension 0, may hold values from -1.75 to 1.75
- embed_table: bfloat16 [32768, 2048], P(None, 'rows'), may hold values from -6 to 6
- qkv_weight: bfloat16 [2048, 3, 2048], P(None, None, 'rows'), may hold values from -0.125 to 0.125
- gate_weight: float32 [16, 128], replicated, may hold values from -6 to 6
- gate_bias: float32 [16], replicated, may hold values from -2 to 3
- norm_gain: float32 [2048], replicated, may hold values from 0.1 to 1.9
- out_weight: bfloat16 [2048, 2048], P(None, 'rows'), may hold values from -0.125 to 0.125
Outputs:
- layer_out: bfloat16 [1, 256, 2048], P(None, 'groups', 'rows'), parts along dimension 1
- final_states: bfloat16 [256, 16, 128, 128], P(('groups', 'rows')), parts along dimension 0
There are 2 independent parts, one for each index of `groups`. A program takes and returns all parts, laid end to end along the dimension named above; an argument that names none is the same for every part. Nothing has to cross between parts.
Inputs may be any that keep to these rules, and one draw needn't show every extreme that they name: The 32 beams of a user fall into 4 aligned blocks of 8. In every step and for every user, at most 2 children of one block have parents in any one other block, and in every step some user has exactly 2 children of one block with parents in another block.
All inputs are finite; a program needn't handle non-finite values.
Results may differ from a plain program's by a relative error of at most 0.0074.
Values may be sent and summed in bfloat16 or wider, within the bound.
A program may use at most 64 MiB of HBM per device.

v0:
```python
import functools
import math

import jax
import jax.numpy as jnp
from jax import lax
from jax.experimental import pallas as pl
from jax.experimental.pallas import tpu as pltpu
from jax.sharding import PartitionSpec as P

CAP = 2
AHEAD, BEHIND, MIDDLE = 3, 2, 7
ANY = pl.BlockSpec(memory_space=pl.ANY)
VM = pl.BlockSpec(memory_space=pltpu.VMEM)
SM = pl.BlockSpec(memory_space=pltpu.SMEM)


def gather_kernel(
    middle, list_ref, tok_ref, state_ref, table_ref, one_ref, far_ref, two_ref, three_ref, out_ref,
    buf, rows_in, wide, rows_out, in_sem, out_sem, row_sem, mid_sem
):
    device = lax.axis_index("rows")
    member, user = device % 4, device // 4
    row_local = state_ref.shape[0]
    loads = []
    for slot in list(range(CAP, 3 * CAP)) + list(range(CAP)):
        partner, order = slot // CAP + 1, slot % CAP
        base = jnp.bitwise_xor(member, partner) * row_local
        seen, chosen = jnp.int32(0), jnp.int32(0)
        for child in range(row_local):
            parent = list_ref[0, user, base + child]
            needed = parent // row_local == member
            chosen = jnp.where(needed & (seen == order), parent % row_local, chosen)
            seen = seen + needed.astype(jnp.int32)
        load = pltpu.make_async_copy(state_ref.at[chosen], buf.at[slot], in_sem.at[slot])
        load.start()
        loads.append((slot, load))
    count = out_ref.shape[0]

    def begin(i, carry):
        pltpu.make_async_copy(table_ref.at[tok_ref[0, i] // 8], rows_in.at[i], row_sem).start()
        return carry

    lax.fori_loop(0, count, begin, 0, unroll=8)
    stores = []
    for slot, load in loads:
        load.wait()
        target = one_ref.at[slot] if slot < CAP else far_ref.at[slot - CAP]
        store = pltpu.make_async_copy(buf.at[slot], target, out_sem.at[slot])
        store.start()
        stores.append(store)
        if slot >= CAP:
            half = (two_ref, three_ref)[slot // CAP - 1]
            store = pltpu.make_async_copy(
                buf.at[slot, pl.ds(*middle)], half.at[slot % CAP], mid_sem.at[slot - CAP]
            )
            store.start()
            stores.append(store)
    pltpu.make_async_copy(table_ref.at[pl.ds(0, count)], rows_in, row_sem).wait()
    wide[...] = rows_in[...].astype(jnp.float32).reshape(wide.shape)

    def pick(i, carry):
        rows_out[pl.ds(i, 1), :] = wide[pl.ds(i * 8 + tok_ref[0, i] % 8, 1), :]
        return carry

    lax.fori_loop(0, count, pick, 0, unroll=8)
    out_ref[...] = rows_out[...].astype(jnp.bfloat16)
    for store in stores:
        store.wait()


def gather(middle, parents, tokens, states, table):
    rest = states.shape[1:]
    slots = 3 * CAP
    count, width = tokens.shape[1], table.shape[1]
    size = slots * math.prod(rest) * 2
    return pl.pallas_call(
        functools.partial(gather_kernel, middle),
        out_shape=(
            jax.ShapeDtypeStruct((CAP,) + rest, states.dtype),
            jax.ShapeDtypeStruct((2 * CAP,) + rest, states.dtype),
            jax.ShapeDtypeStruct((CAP, middle[1]) + rest[1:], states.dtype),
            jax.ShapeDtypeStruct((CAP, middle[1]) + rest[1:], states.dtype),
            jax.ShapeDtypeStruct((count, width), table.dtype),
        ),
        in_specs=[SM, SM, ANY, ANY],
        out_specs=(ANY, ANY, ANY, ANY, VM),
        scratch_shapes=[
            pltpu.VMEM((slots,) + rest, states.dtype),
            pltpu.VMEM((count, 8, width), table.dtype),
            pltpu.VMEM((count * 8, width), jnp.float32),
            pltpu.VMEM((count, width), jnp.float32),
            pltpu.SemaphoreType.DMA((slots,)),
            pltpu.SemaphoreType.DMA((slots,)),
            pltpu.SemaphoreType.DMA,
            pltpu.SemaphoreType.DMA((2 * CAP,)),
        ],
        cost_estimate=pl.CostEstimate(flops=0, bytes_accessed=2 * size, transcendentals=0),
        name="gather_rows",
    )(parents, tokens, states, table.reshape(table.shape[0] // 8, 8, width))


def greet(peers):
    barrier = pltpu.get_barrier_semaphore()
    for peer in peers:
        pl.semaphore_signal(
            barrier, inc=1, device_id={"rows": peer}, device_id_type=pl.DeviceIdType.MESH
        )
    pl.semaphore_wait(barrier, len(peers))


def remote(source, target_ref, out_sem, in_sem, target):
    return pltpu.make_async_remote_copy(
        src_ref=source,
        dst_ref=target_ref,
        send_sem=out_sem,
        recv_sem=in_sem,
        device_id={"rows": target},
        device_id_type=pl.DeviceIdType.MESH,
    )


def neighbours(count):
    me = lax.axis_index("rows")
    member, my_level = me % 4, me // 4
    side_member = (member + 2) % 4
    twin_member = member + 1 - 2 * (member % 2)
    diag_member = (twin_member + 2) % 4
    levels = [(my_level + k) % (count // 4) for k in range(1, count // 4)]
    return me, my_level, member, side_member, twin_member, diag_member, levels


def phase(count, spans, mode, in_ref, out_ref, stage, sems, bulk):
    send_sem, recv_sem, own_sem = sems
    me, my_level, member, side_member, twin_member, diag_member, levels = neighbours(count)
    side, twin, diag = (my_level * 4 + m for m in (side_member, twin_member, diag_member))
    peers = [other * 4 + member for other in levels]
    side_peers = [other * 4 + side_member for other in levels]

    def place(block):
        if mode == "columns":
            return out_ref.at[:, pl.ds(pl.multiple_of(block * spans, spans), spans)]
        return out_ref.at[pl.ds(pl.multiple_of(block * spans, spans), spans)]

    def part(ref, other):
        if mode == "exchange":
            return ref.at[pl.ds(pl.multiple_of(other * spans, spans), spans)]
        return ref

    sent = []

    def send(source, block, target, target_ref=None):
        target_ref = place(block) if target_ref is None else target_ref
        copy = remote(source, target_ref, send_sem.at[len(sent)], recv_sem.at[block], target)
        copy.start()
        sent.append(copy)

    def arrived(block, ref=None):
        ref = place(block) if ref is None else ref
        remote(ref, ref, send_sem.at[0], recv_sem.at[block], twin).wait_recv()

    landing = stage if mode == "exchange" else place(side)
    send(in_ref, me, side, stage if mode == "exchange" else None)
    for other in levels:
        send(part(in_ref, other), me, other * 4 + member)
    send(part(in_ref, my_level), me, twin)
    for copy in bulk:
        copy.start()
    own = pltpu.make_async_copy(part(in_ref, my_level), place(me), own_sem.at[0])
    own.start()
    arrived(side, landing)
    for other in levels:
        send(part(landing, other), side, other * 4 + member)
    send(part(landing, my_level), side, twin)
    if mode == "exchange":
        extra = pltpu.make_async_copy(part(stage, my_level), place(side), own_sem.at[1])
        extra.start()
    for peer in peers + side_peers:
        arrived(peer)
        send(place(peer), peer, twin)
    arrived(twin)
    arrived(diag)
    for other in levels:
        arrived(other * 4 + twin_member)
        arrived(other * 4 + diag_member)
    own.wait()
    if mode == "exchange":
        extra.wait()
    return sent


def far_copies(count, far_ref, got_ref, first, offset, heads, out_sem, in_sem, at):
    _, my_level, _, side_member, _, diag_member, _ = neighbours(count)
    return [
        remote(
            far_ref.at[slot, pl.ds(first + offset, heads)],
            got_ref.at[slot, pl.ds(offset, heads)],
            out_sem.at[at + slot],
            in_sem.at[at + slot],
            my_level * 4 + (side_member if slot < CAP else diag_member),
        )
        for slot in range(2 * CAP)
    ]


def meet(count):
    _, my_level, member, side_member, twin_member, diag_member, levels = neighbours(count)
    greet(
        [my_level * 4 + m for m in (side_member, twin_member, diag_member)]
        + [other * 4 + member for other in levels]
    )


def inputs_kernel(
    count, beams, split, in_ref, weight_ref, far_ref, one_ref, out_ref, got_ref, got_one_ref,
    weights, every, proj, stage, weight_sem, send_a, recv_a, own_a, send_b, recv_b, own_b,
    bulk_send, bulk_recv
):
    column_local = in_ref.shape[1]
    load = pltpu.make_async_copy(weight_ref, weights, weight_sem)
    load.start()
    meet(count)
    _, my_level, _, _, twin_member, _, _ = neighbours(count)
    ahead = far_copies(count, far_ref, got_ref, 0, 0, split[0], bulk_send, bulk_recv, 0)
    behind = far_copies(
        count, far_ref, got_ref, 0, split[0], split[1], bulk_send, bulk_recv, 2 * CAP
    )
    behind.append(
        remote(
            one_ref, got_one_ref, bulk_send.at[4 * CAP], bulk_recv.at[4 * CAP],
            my_level * 4 + twin_member,
        )
    )
    sent = phase(
        count, column_local, "columns", in_ref, every, None, (send_a, recv_a, own_a), ahead
    )
    load.wait()
    for slab in range(3):
        proj[:, slab * column_local : (slab + 1) * column_local] = jnp.dot(
            every[...], weights[slab], preferred_element_type=jnp.float32
        ).astype(jnp.bfloat16)
    sent += phase(count, beams, "exchange", proj, out_ref, stage, (send_b, recv_b, own_b), behind)
    for copy in sent:
        copy.wait_send()
    for copy in ahead + behind:
        copy.wait()


def inputs(local_columns, weights, far, one, count, beams, split):
    row_total, column_local = local_columns.shape
    depth = weights.shape[1]
    sems = [
        pltpu.SemaphoreType.DMA((count - 1,)),
        pltpu.SemaphoreType.DMA((count,)),
        pltpu.SemaphoreType.DMA((2,)),
    ]
    return pl.pallas_call(
        functools.partial(inputs_kernel, count, beams, split),
        out_shape=(
            jax.ShapeDtypeStruct((count * beams, 3 * column_local), jnp.bfloat16),
            jax.ShapeDtypeStruct((far.shape[0], sum(split)) + far.shape[2:], far.dtype),
            jax.ShapeDtypeStruct(one.shape, one.dtype),
        ),
        in_specs=[VM, ANY, ANY, ANY],
        out_specs=(VM, ANY, ANY),
        scratch_shapes=[
            pltpu.VMEM(weights.shape, weights.dtype),
            pltpu.VMEM((row_total, depth), jnp.bfloat16),
            pltpu.VMEM((row_total, 3 * column_local), jnp.bfloat16),
            pltpu.VMEM((row_total, 3 * column_local), jnp.bfloat16),
            pltpu.SemaphoreType.DMA,
        ]
        + sems
        + sems
        + [pltpu.SemaphoreType.DMA((4 * CAP + 1,)), pltpu.SemaphoreType.DMA((4 * CAP + 1,))],
        compiler_params=pltpu.CompilerParams(collective_id=1, has_side_effects=True),
        name="spread_inputs",
    )(local_columns, weights, far, one)


def normed_kernel(
    count, first, heads, in_ref, far_ref, out_ref, got_ref, send_a, recv_a, own_a, bulk_send,
    bulk_recv
):
    meet(count)
    bulk = far_copies(count, far_ref, got_ref, first, 0, heads, bulk_send, bulk_recv, 0)
    sent = phase(
        count, in_ref.shape[0], "rows", in_ref, out_ref, None, (send_a, recv_a, own_a), bulk
    )
    for copy in sent:
        copy.wait_send()
    for copy in bulk:
        copy.wait()


def spread_normed(normed, far, count, first, heads):
    return pl.pallas_call(
        functools.partial(normed_kernel, count, first, heads),
        out_shape=(
            jax.ShapeDtypeStruct((count * normed.shape[0], normed.shape[1]), normed.dtype),
            jax.ShapeDtypeStruct((far.shape[0], heads) + far.shape[2:], far.dtype),
        ),
        in_specs=[VM, ANY],
        out_specs=(VM, ANY),
        scratch_shapes=[
            pltpu.SemaphoreType.DMA((count - 1,)),
            pltpu.SemaphoreType.DMA((count,)),
            pltpu.SemaphoreType.DMA((2,)),
            pltpu.SemaphoreType.DMA((2 * CAP,)),
            pltpu.SemaphoreType.DMA((2 * CAP,)),
        ],
        compiler_params=pltpu.CompilerParams(collective_id=2, has_side_effects=True),
        name="spread_normed",
    )(normed, far)


def read_kernel(
    head_size, bias_ref, qkv_ref, state_ref, weight_ref, gain_ref, owner_ref, slot_ref, out_ref
):
    step = pl.program_id(0)
    group = qkv_ref.shape[0]
    masks = [owner_ref[:, p : p + 1] > 0 for p in range(state_ref.shape[0])]
    for head in range(group):
        block = qkv_ref[head]
        q_half = block[:, :head_size]
        queries = q_half.astype(jnp.float32)
        keys = block[:, head_size : 2 * head_size].astype(jnp.float32)
        values = block[:, 2 * head_size :].astype(jnp.float32)
        logit = jnp.sum(keys * weight_ref[head], axis=-1, keepdims=True) / math.sqrt(head_size)
        decay = jax.nn.sigmoid(logit + bias_ref[step * group + head])
        unit = keys * lax.rsqrt(jnp.sum(keys * keys, axis=-1, keepdims=True) + 1e-06)
        spreadq = jnp.concatenate(
            [jnp.where(mask, queries, 0.0).astype(jnp.bfloat16) for mask in masks], axis=1
        )
        stacked = state_ref[:, head].reshape(state_ref.shape[0] * head_size, head_size)
        total = jnp.dot(spreadq, stacked, preferred_element_type=jnp.float32)
        readout = decay * total + jnp.sum(queries * unit, axis=-1, keepdims=True) * values
        scaled = readout * lax.rsqrt(jnp.mean(readout * readout, axis=-1, keepdims=True) + 1e-05)
        normed = (scaled * gain_ref[head]).astype(jnp.bfloat16)
        picked = jnp.dot(slot_ref[...], normed, preferred_element_type=jnp.float32)
        out_ref[:, head * head_size : (head + 1) * head_size] = picked.astype(jnp.bfloat16)


def read(qkv, states, gate_weight, gate_bias, norm_gain, owner, slot_pick):
    heads, beams, triple = qkv.shape
    row_local, _, head_size, _ = states.shape
    slots = slot_pick.shape[0]
    group = 4 if heads % 4 == 0 else 1
    return pl.pallas_call(
        functools.partial(read_kernel, head_size),
        grid=(heads // group,),
        out_shape=jax.ShapeDtypeStruct((slots, heads * head_size), jnp.bfloat16),
        in_specs=[
            SM,
            pl.BlockSpec((group, beams, triple), lambda h: (h, 0, 0)),
            pl.BlockSpec((row_local, group, head_size, head_size), lambda h: (0, h, 0, 0)),
            pl.BlockSpec((group, 1, head_size), lambda h: (h, 0, 0)),
            pl.BlockSpec((group, 1, head_size), lambda h: (h, 0, 0)),
            pl.BlockSpec((beams, row_local), lambda h: (0, 0)),
            pl.BlockSpec((slots, beams), lambda h: (0, 0)),
        ],
        out_specs=pl.BlockSpec((slots, group * head_size), lambda h: (0, h)),
        cost_estimate=pl.CostEstimate(
            flops=2 * beams * math.prod(states.shape),
            bytes_accessed=2 * math.prod(states.shape),
            transcendentals=0,
        ),
        name="read_heads",
    )(
        gate_bias,
        qkv,
        states,
        gate_weight.reshape(heads, 1, head_size),
        norm_gain.reshape(heads, 1, head_size),
        owner,
        slot_pick,
    )


def update_kernel(
    cuts, kind_ref, index_ref, decay_ref, state_ref, one_ref, two_ref, three_ref, early_ref,
    late_ref, unit_ref, value_ref, out_ref, old, new, in_sem, out_sem
):
    row_local, heads = old.shape[0], old.shape[1]
    for row in range(row_local):
        @pl.when(kind_ref[row] == 0)
        def _():
            pltpu.make_async_copy(
                state_ref.at[index_ref[row]], old.at[row], in_sem.at[row]
            ).start()

        @pl.when(kind_ref[row] == 1)
        def _():
            pltpu.make_async_copy(one_ref.at[index_ref[row]], old.at[row], in_sem.at[row]).start()

        @pl.when(kind_ref[row] > 1)
        def _():
            slot = (kind_ref[row] - 2) * CAP + index_ref[row]
            for cut, piece in ((cuts[0], early_ref), (cuts[2], late_ref)):
                pltpu.make_async_copy(
                    piece.at[slot], old.at[row, pl.ds(*cut)], in_sem.at[row]
                ).start()

        for other, piece in ((2, two_ref), (3, three_ref)):
            @pl.when(kind_ref[row] == other)
            def _():
                pltpu.make_async_copy(
                    piece.at[index_ref[row]], old.at[row, pl.ds(*cuts[1])], in_sem.at[row]
                ).start()

    def step(row, carry):
        pltpu.make_async_copy(state_ref.at[0], old.at[row], in_sem.at[row]).wait()
        columns = jnp.transpose(unit_ref[row])
        values = value_ref[row]
        for head in range(heads):
            fresh = columns[:, head : head + 1] * values[head : head + 1, :]
            prior = old[row, head].astype(jnp.float32)
            new[row, head] = (decay_ref[row, head] * prior + fresh).astype(jnp.bfloat16)
        pltpu.make_async_copy(new.at[row], out_ref.at[row], out_sem.at[row]).start()
        return carry

    lax.fori_loop(0, row_local, step, 0)
    for row in range(row_local):
        pltpu.make_async_copy(new.at[row], out_ref.at[row], out_sem.at[row]).wait()


def update(cuts, kind, index, decay, states, pieces, unit, values):
    row_local = states.shape[0]
    return pl.pallas_call(
        functools.partial(update_kernel, cuts),
        out_shape=jax.ShapeDtypeStruct(states.shape, states.dtype),
        in_specs=[SM, SM, SM, ANY] + [ANY] * len(pieces) + [VM, VM],
        out_specs=ANY,
        scratch_shapes=[
            pltpu.VMEM(states.shape, states.dtype),
            pltpu.VMEM(states.shape, states.dtype),
            pltpu.SemaphoreType.DMA((row_local,)),
            pltpu.SemaphoreType.DMA((row_local,)),
        ],
        cost_estimate=pl.CostEstimate(
            flops=4 * math.prod(states.shape),
            bytes_accessed=4 * math.prod(states.shape),
            transcendentals=0,
        ),
        name="update_states",
    )(kind, index, decay, states, *pieces, unit, values)


def swap(block, partner):
    count = lax.axis_size("rows")
    return lax.ppermute(block, "rows", [(low, low ^ partner) for low in range(count)])


def fast(
    token_ids, parents, states, embed_table, qkv_weight, gate_weight, gate_bias, norm_gain,
    out_weight
):
    row_local, heads, head_size, _ = states.shape
    column_local = embed_table.shape[1]
    row_total = token_ids.shape[1]
    users, beams = parents.shape[1], parents.shape[2]
    count = lax.axis_size("rows")
    device = lax.axis_index("rows")
    member, user = device % 4, device // 4
    slots = 16 * ((row_local + 3 * CAP + 15) // 16)

    split = (heads * AHEAD // 16, heads * BEHIND // 16)
    middle = heads * MIDDLE // 16
    early = sum(split)
    cuts = ((0, early), (early, middle), (early + middle, heads - early - middle))
    one, far, two, three, local_columns = gather(
        cuts[1], parents, token_ids, states, embed_table
    )
    qkv, piece_a, got_one = inputs(
        local_columns, jnp.transpose(qkv_weight, (1, 0, 2)), far, one, count, beams, split
    )
    two, three, qkv, lists = lax.optimization_barrier((two, three, qkv, parents[0]))
    got_two = swap(two, 2)
    got_three = swap(three, 3)
    qkv = qkv.reshape(count, beams, 3 * column_local)

    owner_block = lists // row_local
    blocks = owner_block.reshape(users, 4, row_local)
    at = jnp.arange(row_local, dtype=jnp.int32)
    same = (blocks[..., :, None] == blocks[..., None, :]) & (at[:, None] > at[None, :])
    rank = jnp.sum(same.astype(jnp.int32), axis=-1)
    offset = jnp.bitwise_xor(blocks, jnp.arange(4, dtype=jnp.int32)[None, :, None])
    slot = jnp.where(offset == 0, at[None, None, :], row_local + (offset - 1) * CAP + rank)
    slot = slot.reshape(users, beams)
    my_list = lax.dynamic_index_in_dim(lists, user, 0, keepdims=False)
    my_slot = lax.dynamic_index_in_dim(slot, user, 0, keepdims=False)
    held = my_list // row_local == member
    within = my_list % row_local
    slot_pick = held[None, :] & (my_slot[None, :] == jnp.arange(slots, dtype=jnp.int32)[:, None])
    owner = (held[:, None] & (within[:, None] == at[None, :])).astype(jnp.float32)
    own_slot = lax.dynamic_slice_in_dim(my_slot, member * row_local, row_local, 0)
    own_within = lax.dynamic_slice_in_dim(within, member * row_local, row_local, 0)
    far_row = own_slot >= row_local
    kind = jnp.where(far_row, (own_slot - row_local) // CAP + 1, 0)
    index = jnp.where(far_row, (own_slot - row_local) % CAP, own_within)
    source = (
        (jnp.arange(users, dtype=jnp.int32)[:, None] * 4 + owner_block) * slots + slot
    ).reshape(row_total)
    pick = (source[:, None] == jnp.arange(count * slots, dtype=jnp.int32)[None, :]).astype(
        jnp.bfloat16
    )

    normed = read(
        qkv, states, gate_weight, gate_bias, norm_gain, owner, slot_pick.astype(jnp.bfloat16)
    )
    mine = lax.dynamic_slice_in_dim(qkv, member * row_local, row_local, 1)
    keys = mine[:, :, head_size : 2 * head_size].astype(jnp.float32)
    values = jnp.swapaxes(mine[:, :, 2 * head_size :].astype(jnp.float32), 0, 1)
    logit = jnp.sum(keys * gate_weight[:, None, :], axis=-1) / math.sqrt(head_size)
    decay = jax.nn.sigmoid(logit + gate_bias[:, None]).T
    unit = keys * lax.rsqrt(jnp.sum(keys * keys, axis=-1, keepdims=True) + 1e-06)
    unit = jnp.swapaxes(unit, 0, 1)
    normed, pick, decay, unit, values, kind, index = lax.optimization_barrier(
        (normed, pick, decay, unit, values, kind, index)
    )
    every_normed, piece_c = spread_normed(normed, far, count, *cuts[2])
    ordered = jnp.dot(pick, every_normed, preferred_element_type=jnp.float32)
    attention = jnp.dot(
        ordered.astype(jnp.bfloat16), out_weight, preferred_element_type=jnp.float32
    )
    layer_out = (local_columns.astype(jnp.float32) + attention).astype(jnp.bfloat16)
    state_now = update(
        cuts, kind, index, decay, states,
        (got_one, got_two, got_three, piece_a, piece_c), unit, values
    )
    return (layer_out[None], state_now)


def from_partner(block, axis, stride):
    count = lax.axis_size(axis)
    route = []
    for low in range(count):
        high = low | 1 << stride
        if high != low and high < count:
            route += [(low, high), (high, low)]
    return lax.ppermute(block, axis, route)


def outgoing(state_now, parent_list, member, row_local, partner):
    target = jnp.bitwise_xor(member, partner)
    children = lax.dynamic_slice_in_dim(parent_list, target * row_local, row_local, 0)
    needed = children // row_local == member
    rank_index = jnp.cumsum(needed.astype(jnp.int32)) - 1
    slot_ids = jnp.arange(CAP, dtype=jnp.int32)
    chosen = jnp.sum(
        jnp.where(
            needed[None, :] & (rank_index[None, :] == slot_ids[:, None]),
            (children % row_local)[None, :],
            0,
        ),
        axis=1,
    )
    return jnp.take(state_now, chosen, axis=0)


def route(state_now, parent_list, member, row_local):
    first_out = outgoing(state_now, parent_list, member, row_local, 1)
    second_out = outgoing(state_now, parent_list, member, row_local, 2)
    corner_out = outgoing(state_now, parent_list, member, row_local, 3)
    got_one = from_partner(first_out, "rows", 0)
    got_two = from_partner(second_out, "rows", 1)
    relayed = from_partner(corner_out, "rows", 0)
    got_three = from_partner(relayed, "rows", 1)
    own_list = lax.dynamic_slice_in_dim(parent_list, member * row_local, row_local, 0)
    source = own_list // row_local
    partner = jnp.bitwise_xor(source, member)
    slot_index = jnp.arange(row_local, dtype=jnp.int32)
    earlier = (source[:, None] == source[None, :]) & (slot_index[:, None] > slot_index[None, :])
    rank_index = jnp.sum(earlier.astype(jnp.int32), axis=1)
    position = jnp.where(
        partner == 0, own_list % row_local, row_local + (partner - 1) * CAP + rank_index
    )
    pooled = jnp.concatenate([state_now, got_one, got_two, got_three], 0)
    return jnp.take(pooled, position, axis=0)


def per_device(
    token_ids,
    parents,
    states,
    embed_table,
    qkv_weight,
    gate_weight,
    gate_bias,
    norm_gain,
    out_weight,
):
    row_local = states.shape[0]
    heads = states.shape[1]
    head_size = states.shape[2]
    count = lax.axis_size("rows")
    if (
        embed_table.shape[1] == head_size
        and head_size % 128 == 0
        and count == heads
        and parents.shape[0] == 1
        and parents.shape[2] == 4 * row_local
        and parents.shape[1] * 4 == count
        and parents.shape[2] % 16 == 0
    ):
        return fast(
            token_ids, parents, states, embed_table, qkv_weight, gate_weight, gate_bias,
            norm_gain, out_weight
        )
    width = heads * head_size
    column_local = embed_table.shape[1]
    row_total = token_ids.shape[1]
    device = lax.axis_index("rows")
    member = device % 4
    user_index = device // 4
    weight_flat = qkv_weight.reshape(qkv_weight.shape[0], 3 * column_local)
    local_columns = jnp.take(embed_table, token_ids, axis=0)
    every_proj = jnp.einsum(
        "...rc,cf->...rf",
        lax.all_gather(local_columns, "rows", axis=2, tiled=True),
        weight_flat,
        preferred_element_type=jnp.float32,
    )
    state_now = states
    step_proj = every_proj[0]
    projected = step_proj.astype(jnp.bfloat16).reshape(row_total, 3, column_local)
    mine = lax.all_to_all(projected, "rows", split_axis=0, concat_axis=2, tiled=True)
    queries = mine[:, 0].reshape(row_local, heads, head_size)
    key_float = mine[:, 1].reshape(row_local, heads, head_size).astype(jnp.float32)
    values = mine[:, 2].reshape(row_local, heads, head_size).astype(jnp.float32)
    gate_logit = jnp.sum(key_float * gate_weight, axis=-1) / math.sqrt(head_size) + gate_bias
    decay_rate = jax.nn.sigmoid(gate_logit)
    key_unit = key_float * lax.rsqrt(jnp.sum(key_float * key_float, axis=-1, keepdims=True) + 1e-06)
    parent_list = lax.dynamic_index_in_dim(parents[0], user_index, 0, keepdims=False)
    prior_state = route(state_now, parent_list, member, row_local)
    new_state = (
        decay_rate[:, :, None, None] * prior_state.astype(jnp.float32)
        + key_unit[:, :, :, None] * values[:, :, None, :]
    )
    state_now = new_state.astype(jnp.bfloat16)
    readout = jnp.einsum("rhd,rhde->rhe", queries, state_now, preferred_element_type=jnp.float32)
    scaled = readout * lax.rsqrt(jnp.mean(readout * readout, axis=-1, keepdims=True) + 1e-05)
    normed = (scaled.reshape(row_local, width) * norm_gain).astype(jnp.bfloat16)
    attention = jnp.dot(
        lax.all_gather(normed, "rows", axis=0, tiled=True),
        out_weight,
        preferred_element_type=jnp.float32,
    )
    outputs = [(local_columns[0].astype(jnp.float32) + attention).astype(jnp.bfloat16)]
    return (jnp.stack(outputs), state_now)


def solution(mesh):
    placed = (
        P(None, "groups"),
        P(None, "groups", None),
        P(("groups", "rows"), None, None, None),
        P(None, "rows"),
        P(None, None, "rows"),
        P(),
        P(),
        P(),
        P(None, "rows"),
    )
    return jax.shard_map(
        per_device,
        mesh=mesh,
        in_specs=placed,
        out_specs=(P(None, "groups", "rows"), P(("groups", "rows"), None, None, None)),
        check_vma=False,
    )
```

profile of v0, /device:TPU:0, one launch (start us, length us, event | category | flops | bytes accessed | tf_op | source)
XLA Modules:
  0.0 78.6 jit_solution(6020173685224340165)
XLA Ops:
  0.6 5.3 %gather_rows.1 = (bf16[2,16,128,128]{3,2,1,0:T(8,128)(2,1)}, bf16[4,16,128,128]{3,2,1,0:T(8,128)(2,1)}, bf16[2,7,128,128]{3,2,1,0:T(8,128)(2,1)}, bf16[2,7,128,128]{3,2,1,0:T(8,128)(2,1)}, bf16[128,128]{1,0:T(8,128)(2,1)}) custom-call(s32[1,4,32]{2,1,0:T(4,128)} %list_ref.1, s32[1,128]{1,0:T(1,128)} %tok_ref.1, bf16[8,16,128,128]{3,2,1,0:T(8,128)(2,1)} %state_ref.5, ...), custom_call_target="tpu_custom_call" | custom-call | bytes 6291456 | tf_op jit(solution)/shard_map/gather_rows/pallas_call | solution.py:77
  6.0 26.2 %spread_inputs.1 = (bf16[512,384]{1,0:T(8,128)(2,1)}, bf16[4,5,128,128]{3,2,1,0:T(8,128)(2,1)}, bf16[2,16,128,128]{3,2,1,0:T(8,128)(2,1)}) custom-call(bf16[128,128]{1,0:T(8,128)(2,1)} %get-tuple-element.23.in_ref, bf16[3,2048,128]{2,1,0:T(8,128)(2,1)} %bitcast.56, bf16[4,16,128,128]{3,2,1,0:T(8,128)(2,1)} %get-tuple-element.26.far_ref, ...), custom_call_target="tpu_custom_call" | custom-call | tf_op jit(solution)/shard_map/spread_inputs/pallas_call | solution.py:257
  32.3 0.7 collective-permute-start
  32.9 1.2 %collective-permute-start.1 = (bf16[2,7,128,128]{3,2,1,0:T(8,128)(2,1)S(1)}, bf16[2,7,128,128]{3,2,1,0:T(8,128)(2,1)S(1)}, u32[]{:S(2)}, u32[]{:S(2)}) collective-permute-start(bf16[2,7,128,128]{3,2,1,0:T(8,128)(2,1)S(1)} %copy-done.7), channel_id=1, source_target_pairs={{0,3},{1,2},{2,1},{3,0},{4,7},{5,6},{6,5},{7,4},{8,11},{9,10},{10,... | collective-permute-start | bytes 1376264 | tf_op jit(solution)/shard_map/ppermute | solution.py:451
  34.2 0.1 broadcast_in_dim.16
  34.3 0.1 xor.14
  34.4 0.1 eq.92
  34.5 0.4 convert_reduce_fusion
  34.9 0.1 reduce_sum.30
  35.1 0.1 eq.100
  35.2 0.8 %constant_dynamic-slice_fusion.1 = (bf16[16,8,128]{2,1,0:T(8,128)(2,1)S(1)}, bf16[16,8,128]{2,1,0:T(8,128)(2,1)S(1)}) fusion(bf16[16,32,384]{2,1,0:T(8,128)(2,1)} %bitcast.57, s32[]{:T(128)S(6)} %select_n.83, s32[]{:T(128)S(6)} %add.118, s32[]{:T(128)S(6)} %add.117), kind=kLoop, calls=%fused_computation.51 | loop fusion | bytes 131084 | tf_op jit(solution)/shard_map/slice | solution.py:513
  36.0 0.6 convert_bitcast_fusion.value_ref
  36.7 0.6 fusion.11.slot_ref
  37.3 0.7 fusion.9.owner_ref
  38.0 0.1 fusion.6
  38.1 0.6 divide_bitcast_fusion
  38.7 0.7 bitcast_select_fusion
  39.4 6.8 %read_heads.1.in_ref = bf16[16,2048]{1,0:T(8,128)(2,1)} custom-call(f32[16]{0:T(128)} %bias_ref.1, bf16[16,32,384]{2,1,0:T(8,128)(2,1)} %bitcast.58, bf16[8,16,128,128]{3,2,1,0:T(8,128)(2,1)} %state_ref.5, f32[16,1,128]{2,1,0:T(1,128)} %bitcast.59, f32[16,1,128]{2,1,0:T(1,128)} %bitcast.64, f32[32,8]{1,0:T(8,128)} %fusion.9.owner_ref, ...), custom_call_target="tpu_custom_call" | custom-call | flops 134217728 | bytes 4194304 | tf_op jit(solution)/shard_map/read_heads/pallas_call | solution.py:349
  46.1 0.7 fusion.7.unit_ref
  46.8 21.8 %spread_normed.1 = (bf16[256,2048]{1,0:T(8,128)(2,1)}, bf16[4,4,128,128]{3,2,1,0:T(8,128)(2,1)}) custom-call(bf16[16,2048]{1,0:T(8,128)(2,1)} %read_heads.1.in_ref, bf16[4,16,128,128]{3,2,1,0:T(8,128)(2,1)} %get-tuple-element.26.far_ref), custom_call_target="tpu_custom_call" | custom-call | tf_op jit(solution)/shard_map/spread_normed/pallas_call | solution.py:297
  68.7 2.3 %fusion.3 = bf16[1,128,128]{2,1,0:T(8,128)(2,1)} fusion(bf16[2048,128]{1,0:T(8,128)(2,1)S(1)} %copy-done, bf16[128,256]{1,0:T(8,128)(2,1)S(1)} %fusion.4, bf16[256,2048]{1,0:T(8,128)(2,1)} %get-tuple-element.33, bf16[128,128]{1,0:T(8,128)(2,1)S(1)} %copy-done.3), kind=kOutput, calls=%fused_computation.4 | convolution fusion | flops 201637888 | bytes 1703936 | tf_op jit(solution)/shard_map/dot_general | solution.py:523
  71.0 0.8 copy-done.1
  71.7 0.2 copy-done.2
  71.9 6.7 %update_states.1 = bf16[8,16,128,128]{3,2,1,0:T(8,128)(2,1)} custom-call(s32[8]{0:T(128)} %get-tuple-element.34.kind_ref, s32[8]{0:T(128)} %get-tuple-element.35.index_ref, f32[8,16]{1,0:T(8,128)} %get-tuple-element.36.decay_ref, bf16[8,16,128,128]{3,2,1,0:T(8,128)(2,1)} %state_ref.5, bf16[2,16,128,128]{3,2,1,0:T(8,128)(2,1)} %get-tuple-element.37.one_ref, ...), custom_call_target="tpu_custom_call" | custom-call | flops 8388608 | bytes 8388608 | tf_op jit(solution)/shard_map/update_states/pallas_call | solution.py:429
  (29 shorter events, 0.3 us)
Async XLA Ops:
  0.6 68.0 %copy-start = (bf16[2048,128]{1,0:T(8,128)(2,1)S(1)}, bf16[2048,128]{1,0:T(8,128)(2,1)}, u32[]{:S(2)}) copy-start(bf16[2048,128]{1,0:T(8,128)(2,1)} %param.17) | copy-start | bytes 1572868
  6.0 26.3 %copy-start.8 = (bf16[2,7,128,128]{3,2,1,0:T(8,128)(2,1)S(1)}, bf16[2,7,128,128]{3,2,1,0:T(8,128)(2,1)}, u32[]{:S(2)}) copy-start(bf16[2,7,128,128]{3,2,1,0:T(8,128)(2,1)} %get-tuple-element.38) | copy-start | bytes 1376260
  6.0 27.0 %copy-start.7 = (bf16[2,7,128,128]{3,2,1,0:T(8,128)(2,1)S(1)}, bf16[2,7,128,128]{3,2,1,0:T(8,128)(2,1)}, u32[]{:S(2)}) copy-start(bf16[2,7,128,128]{3,2,1,0:T(8,128)(2,1)} %get-tuple-element.39) | copy-start | bytes 1376260
  6.0 28.2 %copy-start.5 = (s32[1,4,32]{2,1,0:T(4,128)S(1)}, s32[1,4,32]{2,1,0:T(4,128)}, u32[]{:S(2)}) copy-start(s32[1,4,32]{2,1,0:T(4,128)} %list_ref.1) | copy-start | bytes 1540
  6.0 32.0 %copy-start.4 = (f32[16,128]{1,0:T(8,128)S(1)}, f32[16,128]{1,0:T(8,128)}, u32[]{:S(2)}) copy-start(f32[16,128]{1,0:T(8,128)} %param.14) | copy-start | bytes 24580
  6.0 32.1 %copy-start.6 = (f32[16]{0:T(128)S(1)}, f32[16]{0:T(128)}, u32[]{:S(2)}) copy-start(f32[16]{0:T(128)} %bias_ref.1) | copy-start | bytes 196
  32.2 36.4 %copy-start.3 = (bf16[128,128]{1,0:T(8,128)(2,1)S(1)}, bf16[128,128]{1,0:T(8,128)(2,1)}, u32[]{:S(2)}) copy-start(bf16[128,128]{1,0:T(8,128)(2,1)} %get-tuple-element.23.in_ref) | copy-start | bytes 98308
  32.3 38.7 %collective-permute-start = (bf16[2,7,128,128]{3,2,1,0:T(8,128)(2,1)S(1)}, bf16[2,7,128,128]{3,2,1,0:T(8,128)(2,1)S(1)}, u32[]{:S(2)}, u32[]{:S(2)}) collective-permute-start(bf16[2,7,128,128]{3,2,1,0:T(8,128)(2,1)S(1)} %copy-done.8), channel_id=1, source_target_pairs={{0,2},{1,3},{2,0},{3,1},{4,6},{5,7},{6,4},{7,5},{8,10},{9,11},{10,... | collective-permute-start | bytes 1376264 | tf_op jit(solution)/shard_map/ppermute | solution.py:451
  32.9 38.0 %collective-permute-start.1 = (bf16[2,7,128,128]{3,2,1,0:T(8,128)(2,1)S(1)}, bf16[2,7,128,128]{3,2,1,0:T(8,128)(2,1)S(1)}, u32[]{:S(2)}, u32[]{:S(2)}) collective-permute-start(bf16[2,7,128,128]{3,2,1,0:T(8,128)(2,1)S(1)} %copy-done.7), channel_id=1, source_target_pairs={{0,3},{1,2},{2,1},{3,0},{4,7},{5,6},{6,5},{7,4},{8,11},{9,10},{10,... | collective-permute-start | bytes 1376264 | tf_op jit(solution)/shard_map/ppermute | solution.py:451
  71.0 0.8 copy-start.1
  71.0 1.0 %copy-start.2 = (bf16[2,7,128,128]{3,2,1,0:T(8,128)(2,1)}, bf16[2,7,128,128]{3,2,1,0:T(8,128)(2,1)S(1)}, u32[]{:S(2)}) copy-start(bf16[2,7,128,128]{3,2,1,0:T(8,128)(2,1)S(1)} %collective-permute-done.1.three_ref) | copy-start | bytes 1376260
where the time goes:
time: 79.1 us; the launch traced here: 78.6 us
  Pallas kernels  66.8 us (84%)
  other arithmetic  4.62 us (6%)
  matrix products  2.29 us (3%)
  local copies, waits for them, and re-layouts  2.22 us (3%)
  starting transfers between devices  1.87 us (2%)
  between operations  0.81 us (1%)
    pallas_call x1, Pallas kernels, inputs(): pl.pallas_call(functools.partial(inputs_kernel, count, beams, split), out...  26.2 us
    pallas_call x1, Pallas kernels, spread_normed(): pl.pallas_call(functools.partial(normed_kernel, count, first, heads), out...  21.8 us
    pallas_call x1, Pallas kernels, read(): pl.pallas_call(functools.partial(read_kernel, head_size), grid=(heads //...  6.75 us
    pallas_call x1, Pallas kernels, update(): pl.pallas_call(functools.partial(update_kernel, cuts), out_shape=jax.Shap...  6.66 us
    pallas_call x1, Pallas kernels, gather(): pl.pallas_call(functools.partial(gather_kernel, middle), out_shape=(jax.S...  5.32 us
    dot_general x1, matrix products, fast(): jnp.dot(ordered.astype(jnp.bfloat16), out_weight, preferred_element_type=...  2.29 us
    ppermute x2, starting transfers between devices, swap(): lax.ppermute(block, 'rows', [(low, low ^ partner) for low in range(count)])  1.87 us
  transfers between devices with their start and end apart: 2, of which 0 were waited for; matrix products, arithmetic and copies ran while one was open for 10% of the time, Pallas kernels for 36%

commit v1 on v0

v1 whole, which is shorter than its diff:
```python
import functools
import math

import jax
import jax.numpy as jnp
from jax import lax
from jax.experimental import pallas as pl
from jax.experimental.pallas import tpu as pltpu
from jax.sharding import PartitionSpec as P

CAP = 2
SPANS = (1, 3, 4, 8)
ANY = pl.BlockSpec(memory_space=pl.ANY)
VM = pl.BlockSpec(memory_space=pltpu.VMEM)
SM = pl.BlockSpec(memory_space=pltpu.SMEM)


def neighbours(count):
    me = lax.axis_index("rows")
    member, my_level = me % 4, me // 4
    side_member = (member + 2) % 4
    twin_member = member + 1 - 2 * (member % 2)
    diag_member = (twin_member + 2) % 4
    levels = [(my_level + k) % (count // 4) for k in range(1, count // 4)]
    return me, my_level, member, side_member, twin_member, diag_member, levels


def remote(source, target_ref, out_sem, in_sem, target):
    return pltpu.make_async_remote_copy(
        src_ref=source,
        dst_ref=target_ref,
        send_sem=out_sem,
        recv_sem=in_sem,
        device_id={"rows": target},
        device_id_type=pl.DeviceIdType.MESH,
    )


def across(row):
    size = row.shape[1]
    wide = jnp.broadcast_to(row, (size, size))
    here = lax.broadcasted_iota(jnp.int32, (size, size), 0)
    there = lax.broadcasted_iota(jnp.int32, (size, size), 1)
    return jnp.sum(jnp.where(here == there, wide, 0.0), axis=1, keepdims=True)


def layer_kernel(
    count, row_local, cuts, list_s, tok_s, bias_s, list_v, gate_v, gain_v, states, table, weights,
    out_weights, got, got_one, unit_o, value_o, decay_o, layer_o,
    st, sb, tab, wts, owts, wide, rows_f, every, proj, qkv, units, vals, decs, spread, slots,
    normed, unit_v, value_v, decay_v, layer_v, layer_b,
    load_sem, tab_sem, w_sem, o_sem, send_sem, bulk_send, bulk_recv, recv_a, recv_b, recv_c,
    recv_d
):
    me, my_level, member, side_m, twin_m, diag_m, levels = neighbours(count)
    side, twin, diag = (my_level * 4 + m for m in (side_m, twin_m, diag_m))
    heads, head_size = st.shape[1], st.shape[2]
    beams = 4 * row_local
    half = member % 2

    barrier = pltpu.get_barrier_semaphore()
    peers = [side, twin, diag] + [other * 4 + member for other in levels]
    for peer in peers:
        pl.semaphore_signal(
            barrier, inc=1, device_id={"rows": peer}, device_id_type=pl.DeviceIdType.MESH
        )
    state_loads = [
        pltpu.make_async_copy(states.at[row], st.at[row], load_sem.at[row])
        for row in range(row_local)
    ]
    for load in state_loads:
        load.start()
    pieces = tab_sem.shape[0]
    span = tab.shape[0] // pieces
    table_loads = [
        pltpu.make_async_copy(
            table.at[pl.ds(k * span, span)], tab.at[pl.ds(k * span, span)], tab_sem.at[k]
        )
        for k in range(pieces)
    ]
    for load in table_loads:
        load.start()
    weight_load = pltpu.make_async_copy(weights, wts, w_sem.at[0])
    weight_load.start()
    out_load = pltpu.make_async_copy(out_weights, owts, w_sem.at[1])
    out_load.start()

    chosen = []
    for partner in (2, 3, 1):
        target = (side_m, diag_m, twin_m)[(2, 3, 1).index(partner)]
        seen = jnp.int32(0)
        picks = [jnp.int32(0)] * CAP
        for child in range(row_local):
            parent = list_s[0, my_level, target * row_local + child]
            needed = lax.div(parent, row_local) == member
            for order in range(CAP):
                picks[order] = jnp.where(
                    needed & (seen == order), lax.rem(parent, row_local), picks[order]
                )
            seen = seen + needed.astype(jnp.int32)
        chosen += picks
    for load in state_loads:
        load.wait()
    for slot in range(3 * CAP):
        sb[slot] = st[chosen[slot]]
    pl.semaphore_wait(barrier, len(peers))

    sent, arriving = [], []

    def bulk(index):
        first, length = cuts[index]
        for slot in range(2 * CAP):
            at = index * 2 * CAP + slot
            copy = remote(
                sb.at[slot, pl.ds(first, length)], got.at[slot, pl.ds(first, length)],
                bulk_send.at[at], bulk_recv.at[at], side if slot < CAP else diag,
            )
            copy.start()
            arriving.append(copy)

    def send(source, target_ref, sem, target):
        copy = remote(source, target_ref, send_sem.at[len(sent)], sem, target)
        copy.start()
        sent.append(copy)

    def arrived(ref, sem):
        remote(ref, ref, send_sem.at[0], sem, twin).wait_recv()

    bulk(0)
    for load in table_loads:
        load.wait()
    tokens = rows_f.shape[0]

    def fetch(i, carry):
        wide[pl.ds(pl.multiple_of(i * 8, 8), 8), :] = tab[lax.div(tok_s[0, i], 8)].astype(
            jnp.float32
        )
        return carry

    def pick(i, carry):
        rows_f[pl.ds(i, 1), :] = wide[pl.ds(i * 8 + lax.rem(tok_s[0, i], 8), 1), :]
        return carry

    lax.fori_loop(0, tokens, fetch, 0, unroll=8)
    lax.fori_loop(0, tokens, pick, 0, unroll=8)
    every[me] = rows_f[...].astype(jnp.bfloat16)

    mine = every.at[me]
    send(mine, mine, recv_a.at[me], side)
    for other in levels:
        send(mine, mine, recv_a.at[me], other * 4 + member)
    send(mine, mine, recv_a.at[me], twin)
    bulk(1)

    def took(buffer, sems, block):
        arrived(buffer.at[block], sems.at[block])

    def forward(buffer, sems, block, target):
        send(buffer.at[block], buffer.at[block], sems.at[block], target)

    took(every, recv_a, side)
    for other in levels:
        forward(every, recv_a, side, other * 4 + member)
    forward(every, recv_a, side, twin)
    for column in (member, side_m):
        for other in levels:
            took(every, recv_a, other * 4 + column)
            forward(every, recv_a, other * 4 + column, twin)
    took(every, recv_a, twin)
    took(every, recv_a, diag)
    for column in (twin_m, diag_m):
        for other in levels:
            took(every, recv_a, other * 4 + column)

    weight_load.wait()
    lhs = jnp.concatenate([every[k] for k in range(count)], axis=1)
    for slab in range(3):
        done = jnp.dot(lhs, wts[slab], preferred_element_type=jnp.float32)
        done = done.astype(jnp.bfloat16)
        for level in range(count // 4):
            proj[level, :, slab * head_size : (slab + 1) * head_size] = done[
                level * beams : (level + 1) * beams
            ]

    own = proj.at[my_level]
    for other in levels:
        send(proj.at[other], qkv.at[me], recv_b.at[me], other * 4 + member)
    send(own, qkv.at[me], recv_b.at[me], side)
    send(own, qkv.at[me], recv_b.at[me], twin)
    qkv[me] = proj[my_level]
    for other in levels:
        took(qkv, recv_b, other * 4 + member)
        forward(qkv, recv_b, other * 4 + member, side)
        forward(qkv, recv_b, other * 4 + member, twin)
    bulk(2)
    for level in [my_level] + levels:
        took(qkv, recv_b, level * 4 + side_m)
        forward(qkv, recv_b, level * 4 + side_m, twin)

    lists = list_v[0, pl.ds(my_level, 1), :].astype(jnp.float32)
    place_row = lax.broadcasted_iota(jnp.int32, (1, beams), 1)
    place_col = lax.broadcasted_iota(jnp.int32, (beams, 1), 0)
    lists_row = lists.astype(jnp.int32)
    lists_col = across(lists).astype(jnp.int32)
    block_row, block_col = lax.div(place_row, row_local), lax.div(place_col, row_local)
    from_row, from_col = lax.div(lists_row, row_local), lax.div(lists_col, row_local)
    same = (block_row == block_col) & (from_row == from_col)
    rank_col = jnp.sum(
        jnp.where(same & (place_row < place_col), 1.0, 0.0), axis=1, keepdims=True
    ).astype(jnp.int32)
    rank_row = jnp.sum(
        jnp.where(same & (place_col < place_row), 1.0, 0.0), axis=0, keepdims=True
    ).astype(jnp.int32)
    off_row = jnp.bitwise_xor(block_row, from_row)
    off_col = jnp.bitwise_xor(block_col, from_col)
    slot_row = jnp.where(
        off_row == 0, lax.rem(place_row, row_local), row_local + (off_row - 1) * CAP + rank_row
    )
    slot_col = jnp.where(
        off_col == 0, lax.rem(place_col, row_local), row_local + (off_col - 1) * CAP + rank_col
    )
    slot_count = slots.shape[1]
    slot_index = lax.broadcasted_iota(jnp.int32, (slot_count, beams), 0)
    slot_pick = jnp.where(
        (from_row == member) & (slot_row == slot_index), 1.0, 0.0
    ).astype(jnp.bfloat16)
    wanted = from_col * slot_count + slot_col
    all_slots = lax.broadcasted_iota(jnp.int32, (beams, 4 * slot_count), 1)
    row_pick = jnp.where(wanted == all_slots, 1.0, 0.0)
    row_pick = jnp.concatenate(
        [
            row_pick[m * row_local : (m + 1) * row_local]
            for m in (0, 2, 1, 3)
        ],
        axis=0,
    ).astype(jnp.bfloat16)
    held = jnp.broadcast_to(from_col == member, (beams, head_size))
    within = jnp.broadcast_to(lax.rem(lists_col, row_local), (beams, head_size))
    masks = [held & (within == p) for p in range(row_local)]

    for column in (twin_m, diag_m):
        for level in [my_level] + levels:
            took(qkv, recv_b, level * 4 + column)
    for slot in range(CAP):
        copy = remote(
            sb.at[2 * CAP + slot], got_one.at[slot],
            bulk_send.at[len(cuts) * 2 * CAP + slot], bulk_recv.at[len(cuts) * 2 * CAP + slot],
            twin,
        )
        copy.start()
        arriving.append(copy)

    for head in range(heads):
        block = qkv[head]
        queries = block[:, :head_size].astype(jnp.float32)
        keys = block[:, head_size : 2 * head_size].astype(jnp.float32)
        values = block[:, 2 * head_size :].astype(jnp.float32)
        logit = jnp.sum(keys * gate_v[head : head + 1], axis=-1, keepdims=True)
        decay = jax.nn.sigmoid(logit / math.sqrt(head_size) + bias_s[head])
        unit = keys * lax.rsqrt(jnp.sum(keys * keys, axis=-1, keepdims=True) + 1e-06)
        spreadq = jnp.concatenate(
            [jnp.where(mask, queries, 0.0).astype(jnp.bfloat16) for mask in masks], axis=1
        )
        stacked = st[:, head].reshape(row_local * head_size, head_size)
        total = jnp.dot(spreadq, stacked, preferred_element_type=jnp.float32)
        readout = decay * total + jnp.sum(queries * unit, axis=-1, keepdims=True) * values
        scaled = readout * lax.rsqrt(jnp.mean(readout * readout, axis=-1, keepdims=True) + 1e-05)
        spread[:, head * head_size : (head + 1) * head_size] = (
            scaled * gain_v[head : head + 1]
        ).astype(jnp.bfloat16)
        units[head] = unit
        vals[head] = values
        decs[head] = jnp.broadcast_to(decay, (beams, head_size))
    slots[member] = jnp.dot(
        slot_pick, spread[...], preferred_element_type=jnp.float32
    ).astype(jnp.bfloat16)

    forward(slots, recv_c, member, side)
    forward(slots, recv_c, member, twin)
    bulk(3)
    for head in range(heads):
        here = pl.ds(pl.multiple_of(member * row_local, row_local), row_local)
        for target, source in ((unit_v, units), (value_v, vals), (decay_v, decs)):
            target[:, head : head + 1, :] = source[head, here, :].reshape(
                row_local, 1, head_size
            )
    took(slots, recv_c, side_m)
    forward(slots, recv_c, side_m, twin)
    took(slots, recv_c, twin_m)
    took(slots, recv_c, diag_m)
    level_rows = jnp.dot(
        row_pick, slots[...].reshape(4 * slot_count, heads * head_size),
        preferred_element_type=jnp.float32,
    ).astype(jnp.bfloat16)
    for core in range(2):
        normed[my_level * 2 + core] = level_rows[core * 2 * row_local : (core + 1) * 2 * row_local]
    for other in levels:
        forward(normed, recv_d, my_level * 2 + half, other * 4 + member)
    for other in levels:
        took(normed, recv_d, other * 2 + half)
        forward(normed, recv_d, other * 2 + half, twin)
    for other in levels:
        took(normed, recv_d, other * 2 + 1 - half)
    out_load.wait()
    attention = jnp.dot(
        normed[...].reshape(count * row_local, heads * head_size), owts[...],
        preferred_element_type=jnp.float32,
    )
    for level in range(count // 4):
        for core in range(2):
            for line in range(2):
                source = ((level * 2 + core) * 2 + line) * row_local
                target = ((level * 2 + line) * 2 + core) * row_local
                rows = slice(target, target + row_local)
                layer_v[rows] = rows_f[rows] + attention[source : source + row_local]
    layer_b[...] = layer_v[...].astype(jnp.bfloat16)
    outs = [
        pltpu.make_async_copy(source, target, o_sem.at[k])
        for k, (source, target) in enumerate(
            (
                (unit_v, unit_o), (value_v, value_o), (decay_v, decay_o), (layer_b, layer_o)
            )
        )
    ]
    for copy in sent:
        copy.wait_send()
    for copy in outs:
        copy.start()
    for copy in arriving:
        copy.wait()
    for copy in outs:
        copy.wait()


def layer(
    parents, tokens, gate_bias, gate_weight, norm_gain, states, table, weights, out_weight, count
):
    row_local, heads, head_size, _ = states.shape
    row_total, depth = tokens.shape[1], weights.shape[1]
    beams = parents.shape[2]
    slot_count = 16 * ((row_local + 3 * CAP + 15) // 16)
    cuts, first = [], 0
    for span in SPANS:
        cuts.append((first, span * heads // 16))
        first += span * heads // 16
    bulk = (len(cuts) * 2 + 1) * CAP
    sends = 64
    bf, f32 = jnp.bfloat16, jnp.float32
    dma = pltpu.SemaphoreType.DMA
    rows = (row_local, heads, head_size)
    return pl.pallas_call(
        functools.partial(layer_kernel, count, row_local, tuple(cuts)),
        out_shape=(
            jax.ShapeDtypeStruct((2 * CAP,) + states.shape[1:], states.dtype),
            jax.ShapeDtypeStruct((CAP,) + states.shape[1:], states.dtype),
            jax.ShapeDtypeStruct(rows, f32),
            jax.ShapeDtypeStruct(rows, f32),
            jax.ShapeDtypeStruct(rows, f32),
            jax.ShapeDtypeStruct((row_total, head_size), bf),
        ),
        in_specs=[SM, SM, SM, VM, VM, VM, ANY, ANY, ANY, ANY],
        out_specs=(ANY,) * 6,
        scratch_shapes=[
            pltpu.VMEM(states.shape, bf),
            pltpu.VMEM((3 * CAP,) + states.shape[1:], bf),
            pltpu.VMEM((table.shape[0] // 8, 8, head_size), bf),
            pltpu.VMEM(weights.shape, bf),
            pltpu.VMEM(out_weight.shape, bf),
            pltpu.VMEM((row_total * 8, head_size), f32),
            pltpu.VMEM((row_total, head_size), f32),
            pltpu.VMEM((count, row_total, head_size), bf),
            pltpu.VMEM((count // 4, beams, 3 * head_size), bf),
            pltpu.VMEM((count, beams, 3 * head_size), bf),
            pltpu.VMEM((heads, beams, head_size), f32),
            pltpu.VMEM((heads, beams, head_size), f32),
            pltpu.VMEM((heads, beams, head_size), f32),
            pltpu.VMEM((beams, heads * head_size), bf),
            pltpu.VMEM((4, slot_count, heads * head_size), bf),
            pltpu.VMEM((count // 2, 2 * row_local, heads * head_size), bf),
            pltpu.VMEM(rows, f32),
            pltpu.VMEM(rows, f32),
            pltpu.VMEM(rows, f32),
            pltpu.VMEM((row_total, head_size), f32),
            pltpu.VMEM((row_total, head_size), bf),
            dma((row_local,)),
            dma((4,)),
            dma((2,)),
            dma((4,)),
            dma((sends,)),
            dma((bulk,)),
            dma((bulk,)),
            dma((count,)),
            dma((count,)),
            dma((4,)),
            dma((count // 2,)),
        ],
        compiler_params=pltpu.CompilerParams(collective_id=1, has_side_effects=True),
        name="layer_step",
    )(
        parents, tokens, gate_bias, parents, gate_weight, norm_gain.reshape(heads, head_size),
        states, table.reshape(table.shape[0] // 8, 8, head_size), weights, out_weight,
    )


def update_kernel(
    list_s, states, got, got_one, units, values, decays, layer_in, out_ref, layer_out,
    old, new, unit_v, value_v, decay_v, layer_v, in_sem, out_sem, side_sem
):
    row_local, heads = old.shape[0], old.shape[1]
    device = lax.axis_index("rows")
    member, user = device % 4, device // 4
    sides = [
        pltpu.make_async_copy(source, target, side_sem.at[k])
        for k, (source, target) in enumerate(
            ((units, unit_v), (values, value_v), (decays, decay_v), (layer_in, layer_v))
        )
    ]
    for copy in sides:
        copy.start()
    parents = [list_s[0, user, member * row_local + row] for row in range(row_local)]
    blocks = [lax.div(parent, row_local) for parent in parents]
    for row in range(row_local):
        partner = jnp.bitwise_xor(blocks[row], member)
        rank = jnp.int32(0)
        for earlier in range(row):
            rank = rank + (blocks[earlier] == blocks[row]).astype(jnp.int32)

        @pl.when(partner == 0)
        def _():
            pltpu.make_async_copy(
                states.at[lax.rem(parents[row], row_local)], old.at[row], in_sem.at[row]
            ).start()

        @pl.when(partner == 1)
        def _():
            pltpu.make_async_copy(got_one.at[rank], old.at[row], in_sem.at[row]).start()

        @pl.when(partner > 1)
        def _():
            pltpu.make_async_copy(
                got.at[(partner - 2) * CAP + rank], old.at[row], in_sem.at[row]
            ).start()

    for copy in sides:
        copy.wait()
    last = pltpu.make_async_copy(layer_v, layer_out, side_sem.at[0])
    last.start()

    def step(row, carry):
        pltpu.make_async_copy(states.at[0], old.at[row], in_sem.at[row]).wait()
        columns = jnp.transpose(unit_v[row])
        value = value_v[row]
        decay = decay_v[row]
        for head in range(heads):
            fresh = columns[:, head : head + 1] * value[head : head + 1, :]
            prior = old[row, head].astype(jnp.float32)
            new[row, head] = (decay[head : head + 1, :] * prior + fresh).astype(jnp.bfloat16)
        pltpu.make_async_copy(new.at[row], out_ref.at[row], out_sem.at[row]).start()
        return carry

    lax.fori_loop(0, row_local, step, 0)
    for row in range(row_local):
        pltpu.make_async_copy(new.at[row], out_ref.at[row], out_sem.at[row]).wait()
    last.wait()


def update(parents, states, got, got_one, units, values, decays, layer_in):
    row_local = states.shape[0]
    return pl.pallas_call(
        update_kernel,
        out_shape=(
            jax.ShapeDtypeStruct(states.shape, states.dtype),
            jax.ShapeDtypeStruct(layer_in.shape, layer_in.dtype),
        ),
        in_specs=[SM] + [ANY] * 7,
        out_specs=(ANY, ANY),
        scratch_shapes=[
            pltpu.VMEM(states.shape, states.dtype),
            pltpu.VMEM(states.shape, states.dtype),
            pltpu.VMEM(units.shape, units.dtype),
            pltpu.VMEM(values.shape, values.dtype),
            pltpu.VMEM(decays.shape, decays.dtype),
            pltpu.VMEM(layer_in.shape, layer_in.dtype),
            pltpu.SemaphoreType.DMA((row_local,)),
            pltpu.SemaphoreType.DMA((row_local,)),
            pltpu.SemaphoreType.DMA((4,)),
        ],
        cost_estimate=pl.CostEstimate(
            flops=4 * math.prod(states.shape),
            bytes_accessed=4 * math.prod(states.shape),
            transcendentals=0,
        ),
        name="update_states",
    )(parents, states, got, got_one, units, values, decays, layer_in)


def fast(
    token_ids, parents, states, embed_table, qkv_weight, gate_weight, gate_bias, norm_gain,
    out_weight
):
    count = lax.axis_size("rows")
    got, got_one, units, values, decays, layer_mid = layer(
        parents, token_ids, gate_bias, gate_weight, norm_gain, states, embed_table,
        jnp.transpose(qkv_weight, (1, 0, 2)), out_weight, count,
    )
    state_now, layer_out = update(
        parents, states, got, got_one, units, values, decays, layer_mid
    )
    return (layer_out[None], state_now)


def from_partner(block, axis, stride):
    count = lax.axis_size(axis)
    route = []
    for low in range(count):
        high = low | 1 << stride
        if high != low and high < count:
            route += [(low, high), (high, low)]
    return lax.ppermute(block, axis, route)


def outgoing(state_now, parent_list, member, row_local, partner):
    target = jnp.bitwise_xor(member, partner)
    children = lax.dynamic_slice_in_dim(parent_list, target * row_local, row_local, 0)
    needed = children // row_local == member
    rank_index = jnp.cumsum(needed.astype(jnp.int32)) - 1
    slot_ids = jnp.arange(CAP, dtype=jnp.int32)
    chosen = jnp.sum(
        jnp.where(
            needed[None, :] & (rank_index[None, :] == slot_ids[:, None]),
            (children % row_local)[None, :],
            0,
        ),
        axis=1,
    )
    return jnp.take(state_now, chosen, axis=0)


def route(state_now, parent_list, member, row_local):
    first_out = outgoing(state_now, parent_list, member, row_local, 1)
    second_out = outgoing(state_now, parent_list, member, row_local, 2)
    corner_out = outgoing(state_now, parent_list, member, row_local, 3)
    got_one = from_partner(first_out, "rows", 0)
    got_two = from_partner(second_out, "rows", 1)
    relayed = from_partner(corner_out, "rows", 0)
    got_three = from_partner(relayed, "rows", 1)
    own_list = lax.dynamic_slice_in_dim(parent_list, member * row_local, row_local, 0)
    source = own_list // row_local
    partner = jnp.bitwise_xor(source, member)
    slot_index = jnp.arange(row_local, dtype=jnp.int32)
    earlier = (source[:, None] == source[None, :]) & (slot_index[:, None] > slot_index[None, :])
    rank_index = jnp.sum(earlier.astype(jnp.int32), axis=1)
    position = jnp.where(
        partner == 0, own_list % row_local, row_local + (partner - 1) * CAP + rank_index
    )
    pooled = jnp.concatenate([state_now, got_one, got_two, got_three], 0)
    return jnp.take(pooled, position, axis=0)


def per_device(
    token_ids,
    parents,
    states,
    embed_table,
    qkv_weight,
    gate_weight,
    gate_bias,
    norm_gain,
    out_weight,
):
    row_local = states.shape[0]
    heads = states.shape[1]
    head_size = states.shape[2]
    count = lax.axis_size("rows")
    if (
        embed_table.shape[1] == head_size
        and head_size % 128 == 0
        and count == heads
        and parents.shape[0] == 1
        and parents.shape[2] == 4 * row_local
        and parents.shape[1] * 4 == count
        and row_local % 8 == 0
        and heads % 16 == 0
        and math.prod(embed_table.shape) * 2 <= 1 << 24
        and math.prod(states.shape) * 2 <= 1 << 23
    ):
        return fast(
            token_ids, parents, states, embed_table, qkv_weight, gate_weight, gate_bias,
            norm_gain, out_weight
        )
    width = heads * head_size
    column_local = embed_table.shape[1]
    row_total = token_ids.shape[1]
    device = lax.axis_index("rows")
    member = device % 4
    user_index = device // 4
    weight_flat = qkv_weight.reshape(qkv_weight.shape[0], 3 * column_local)
    local_columns = jnp.take(embed_table, token_ids, axis=0)
    every_proj = jnp.einsum(
        "...rc,cf->...rf",
        lax.all_gather(local_columns, "rows", axis=2, tiled=True),
        weight_flat,
        preferred_element_type=jnp.float32,
    )
    state_now = states
    step_proj = every_proj[0]
    projected = step_proj.astype(jnp.bfloat16).reshape(row_total, 3, column_local)
    mine = lax.all_to_all(projected, "rows", split_axis=0, concat_axis=2, tiled=True)
    queries = mine[:, 0].reshape(row_local, heads, head_size)
    key_float = mine[:, 1].reshape(row_local, heads, head_size).astype(jnp.float32)
    values = mine[:, 2].reshape(row_local, heads, head_size).astype(jnp.float32)
    gate_logit = jnp.sum(key_float * gate_weight, axis=-1) / math.sqrt(head_size) + gate_bias
    decay_rate = jax.nn.sigmoid(gate_logit)
    key_unit = key_float * lax.rsqrt(jnp.sum(key_float * key_float, axis=-1, keepdims=True) + 1e-06)
    parent_list = lax.dynamic_index_in_dim(parents[0], user_index, 0, keepdims=False)
    prior_state = route(state_now, parent_list, member, row_local)
    new_state = (
        decay_rate[:, :, None, None] * prior_state.astype(jnp.float32)
        + key_unit[:, :, :, None] * values[:, :, None, :]
    )
    state_now = new_state.astype(jnp.bfloat16)
    readout = jnp.einsum("rhd,rhde->rhe", queries, state_now, preferred_element_type=jnp.float32)
    scaled = readout * lax.rsqrt(jnp.mean(readout * readout, axis=-1, keepdims=True) + 1e-05)
    normed = (scaled.reshape(row_local, width) * norm_gain).astype(jnp.bfloat16)
    attention = jnp.dot(
        lax.all_gather(normed, "rows", axis=0, tiled=True),
        out_weight,
        preferred_element_type=jnp.float32,
    )
    outputs = [(local_columns[0].astype(jnp.float32) + attention).astype(jnp.bfloat16)]
    return (jnp.stack(outputs), state_now)


def solution(mesh):
    placed = (
        P(None, "groups"),
        P(None, "groups", None),
        P(("groups", "rows"), None, None, None),
        P(None, "rows"),
        P(None, None, "rows"),
        P(),
        P(),
        P(),
        P(None, "rows"),
    )
    return jax.shard_map(
        per_device,
        mesh=mesh,
        in_specs=placed,
        out_specs=(P(None, "groups", "rows"), P(("groups", "rows"), None, None, None)),
        check_vma=False,
    )
```

time: 79.1 us -> 71.1 us (0.90)
  other arithmetic: 4.62 us -> 0 us
  Pallas kernels: 66.8 us -> 70.2 us
  matrix products: 2.29 us -> 0 us
  local copies, waits for them, and re-layouts: 2.22 us -> 0 us
  starting transfers between devices: 1.87 us -> 0 us
    pallas_call x5 -> x2, Pallas kernels: 66.8 us -> 70.2 us  [the longest x1 62.8 us: layer(): pl.pallas_call(functools.partial(layer_kernel, count, row_local, tuple(cu...]
    dot_general x1 -> x0, matrix products: 2.29 us -> none  [fast(): jnp.dot(ordered.astype(jnp.bfloat16), out_weight, preferred_element_type=...]
    ppermute x2 -> x0, starting transfers between devices: 1.87 us -> none  [swap(): lax.ppermute(block, 'rows', [(low, low ^ partner) for low in range(count)])]
    convert_element_type x3 -> x0, other arithmetic: 1.35 us -> none  [the longest x1 0.67 us: fast(): (held[:, None] & (within[:, None] == at[None, :])).astype(jnp.float32)]
    transpose x2 -> x0, other arithmetic: 1.32 us -> none  [the longest x1 0.7 us: fast(): unit = jnp.swapaxes(unit, 0, 1)]
    unnamed x18 -> x0, local copies, waits for them, and re-layouts: 0.99 us -> none
  transfers between devices with their start and end apart: 2 -> 0, of which waited for: 0 -> 0; matrix products, arithmetic and copies ran while one was open for 10% -> 0% of each run, Pallas kernels for 36% -> 0%
where the time goes in v1:
time: 71.1 us; the launch traced here: 70.9 us
  Pallas kernels  70.2 us (99%)
    pallas_call x1, Pallas kernels, layer(): pl.pallas_call(functools.partial(layer_kernel, count, row_local, tuple(cu...  62.8 us
    pallas_call x1, Pallas kernels, update(): pl.pallas_call(update_kernel, out_shape=(jax.ShapeDtypeStruct(states.shap...  7.48 us

profile of v1, /device:TPU:0, one launch (start us, length us, event | category | flops | bytes accessed | tf_op | source)
XLA Modules:
  0.0 70.9 jit_solution(6135228016495492121)
XLA Ops:
  0.6 62.8 %layer_step.1 = (bf16[4,16,128,128]{3,2,1,0:T(8,128)(2,1)}, bf16[2,16,128,128]{3,2,1,0:T(8,128)(2,1)}, f32[8,16,128]{2,1,0:T(8,128)}, f32[8,16,128]{2,1,0:T(8,12...) custom-call(s32[1,4,32]{2,1,0:T(4,128)} %list_s.3, s32[1,128]{1,0:T(1,128)} %tok_s.1, f32[16]{0:T(128)} %bias_s.1, ...), custom_call_target="tpu_custom_call" | custom-call | tf_op jit(solution)/shard_map/layer_step/pallas_call | solution.py:351
  63.4 7.5 %update_states.1 = (bf16[8,16,128,128]{3,2,1,0:T(8,128)(2,1)}, bf16[128,128]{1,0:T(8,128)(2,1)}) custom-call(s32[1,4,32]{2,1,0:T(4,128)} %list_s.3, bf16[8,16,128,128]{3,2,1,0:T(8,128)(2,1)} %states.3, bf16[4,16,128,128]{3,2,1,0:T(8,128)(2,1)} %get-tuple-element.10.got, bf16[2,16,128,128]{3,2,1,0:T(8,128)(2,1)} %get-tuple-element.11.got_one, ...), custom_call_target="tpu_custom_call" | custom-call | flops 8388608 | bytes 8388608 | tf_op jit(solution)/shard_map/update_states/pallas_call | solution.py:469

commit v2 on v1

--- a/solution.py
+++ b/solution.py
@@ -9,7 +9,7 @@
 from jax.sharding import PartitionSpec as P
 
 CAP = 2
-SPANS = (1, 3, 4, 8)
+SPANS = (2, 5, 3, 6)
 ANY = pl.BlockSpec(memory_space=pl.ANY)
 VM = pl.BlockSpec(memory_space=pltpu.VMEM)
 SM = pl.BlockSpec(memory_space=pltpu.SMEM)
@@ -47,7 +47,7 @@
 def layer_kernel(
     count, row_local, cuts, list_s, tok_s, bias_s, list_v, gate_v, gain_v, states, table, weights,
     out_weights, got, got_one, unit_o, value_o, decay_o, layer_o,
-    st, sb, tab, wts, owts, wide, rows_f, every, proj, qkv, units, vals, decs, spread, slots,
+    first_heads, st, sb, tab, wts, owts, wide, rows_f, every, proj, qkv, units, vals, decs, spread, slots,
     normed, unit_v, value_v, decay_v, layer_v, layer_b,
     load_sem, tab_sem, w_sem, o_sem, send_sem, bulk_send, bulk_recv, recv_a, recv_b, recv_c,
     recv_d
@@ -64,12 +64,15 @@
         pl.semaphore_signal(
             barrier, inc=1, device_id={"rows": peer}, device_id_type=pl.DeviceIdType.MESH
         )
+    early = cuts[0][1]
     state_loads = [
-        pltpu.make_async_copy(states.at[row], st.at[row], load_sem.at[row])
-        for row in range(row_local)
+        pltpu.make_async_copy(
+            states.at[:, pl.ds(first, length)], into, load_sem.at[k]
+        )
+        for k, (first, length, into) in enumerate(
+            ((0, early, first_heads), (0, heads, st))
+        )
     ]
-    for load in state_loads:
-        load.start()
     pieces = tab_sem.shape[0]
     span = tab.shape[0] // pieces
     table_loads = [
@@ -78,12 +81,10 @@
         )
         for k in range(pieces)
     ]
-    for load in table_loads:
+    weight_load = pltpu.make_async_copy(weights, wts, w_sem.at[0])
+    out_load = pltpu.make_async_copy(out_weights, owts, w_sem.at[1])
+    for load in state_loads[:1] + table_loads + state_loads[1:] + [weight_load, out_load]:
         load.start()
-    weight_load = pltpu.make_async_copy(weights, wts, w_sem.at[0])
-    weight_load.start()
-    out_load = pltpu.make_async_copy(out_weights, owts, w_sem.at[1])
-    out_load.start()
 
     chosen = []
     for partner in (2, 3, 1):
@@ -99,10 +100,9 @@
                 )
             seen = seen + needed.astype(jnp.int32)
         chosen += picks
-    for load in state_loads:
-        load.wait()
-    for slot in range(3 * CAP):
-        sb[slot] = st[chosen[slot]]
+    state_loads[0].wait()
+    for slot in range(2 * CAP):
+        sb[slot, :early] = first_heads[chosen[slot]]
     pl.semaphore_wait(barrier, len(peers))
 
     sent, arriving = [], []
@@ -150,6 +150,11 @@
     for other in levels:
         send(mine, mine, recv_a.at[me], other * 4 + member)
     send(mine, mine, recv_a.at[me], twin)
+    state_loads[1].wait()
+    for slot in range(2 * CAP):
+        sb[slot, early:] = st[chosen[slot], early:]
+    for slot in range(2 * CAP, 3 * CAP):
+        sb[slot] = st[chosen[slot]]
     bulk(1)
 
     def took(buffer, sems, block):
@@ -361,6 +366,7 @@
         in_specs=[SM, SM, SM, VM, VM, VM, ANY, ANY, ANY, ANY],
         out_specs=(ANY,) * 6,
         scratch_shapes=[
+            pltpu.VMEM((row_local, cuts[0][1]) + states.shape[2:], bf),
             pltpu.VMEM(states.shape, bf),
             pltpu.VMEM((3 * CAP,) + states.shape[1:], bf),
             pltpu.VMEM((table.shape[0] // 8, 8, head_size), bf),
@@ -382,7 +388,7 @@
             pltpu.VMEM(rows, f32),
             pltpu.VMEM((row_total, head_size), f32),
             pltpu.VMEM((row_total, head_size), bf),
-            dma((row_local,)),
+            dma((2,)),
             dma((4,)),
             dma((2,)),
             dma((4,)),

time: 71.1 us -> 66.2 us (0.931)
  Pallas kernels: 70.2 us -> 64.9 us
    pallas_call x1, Pallas kernels: 62.8 us -> 57.5 us  [layer(): pl.pallas_call(functools.partial(layer_kernel, count, row_local, tuple(cu...]
where the time goes in v2:
time: 66.2 us; the launch traced here: 65.6 us
  Pallas kernels  64.9 us (98%)
    pallas_call x1, Pallas kernels, layer(): pl.pallas_call(functools.partial(layer_kernel, count, row_local, tuple(cu...  57.5 us
    pallas_call x1, Pallas kernels, update(): pl.pallas_call(update_kernel, out_shape=(jax.ShapeDtypeStruct(states.shap...  7.48 us

profile of v2, /device:TPU:0, one launch (start us, length us, event | category | flops | bytes accessed | tf_op | source)
XLA Modules:
  0.0 65.6 jit_solution(11562145384205265235)
XLA Ops:
  0.6 57.5 %layer_step.1 = (bf16[4,16,128,128]{3,2,1,0:T(8,128)(2,1)}, bf16[2,16,128,128]{3,2,1,0:T(8,128)(2,1)}, f32[8,16,128]{2,1,0:T(8,128)}, f32[8,16,128]{2,1,0:T(8,12...) custom-call(s32[1,4,32]{2,1,0:T(4,128)} %list_s.3, s32[1,128]{1,0:T(1,128)} %tok_s.1, f32[16]{0:T(128)} %bias_s.1, ...), custom_call_target="tpu_custom_call" | custom-call | tf_op jit(solution)/shard_map/layer_step/pallas_call | solution.py:356
  58.1 7.5 %update_states.1 = (bf16[8,16,128,128]{3,2,1,0:T(8,128)(2,1)}, bf16[128,128]{1,0:T(8,128)(2,1)}) custom-call(s32[1,4,32]{2,1,0:T(4,128)} %list_s.3, bf16[8,16,128,128]{3,2,1,0:T(8,128)(2,1)} %states.3, bf16[4,16,128,128]{3,2,1,0:T(8,128)(2,1)} %get-tuple-element.10.got, bf16[2,16,128,128]{3,2,1,0:T(8,128)(2,1)} %get-tuple-element.11.got_one, ...), custom_call_target="tpu_custom_call" | custom-call | flops 8388608 | bytes 8388608 | tf_op jit(solution)/shard_map/update_states/pallas_call | solution.py:475

commit v3 on v2

--- a/solution.py
+++ b/solution.py
@@ -9,7 +9,8 @@
 from jax.sharding import PartitionSpec as P
 
 CAP = 2
-SPANS = (2, 5, 3, 6)
+SPANS = (2, 5, 3, 3, 3)
+LAYER_VMEM, UPDATE_VMEM = 44 << 20, 8 << 20
 ANY = pl.BlockSpec(memory_space=pl.ANY)
 VM = pl.BlockSpec(memory_space=pltpu.VMEM)
 SM = pl.BlockSpec(memory_space=pltpu.SMEM)
@@ -46,15 +47,17 @@
 
 def layer_kernel(
     count, row_local, cuts, list_s, tok_s, bias_s, list_v, gate_v, gain_v, states, table, weights,
-    out_weights, got, got_one, unit_o, value_o, decay_o, layer_o,
-    first_heads, st, sb, tab, wts, owts, wide, rows_f, every, proj, qkv, units, vals, decs, spread, slots,
-    normed, unit_v, value_v, decay_v, layer_v, layer_b,
-    load_sem, tab_sem, w_sem, o_sem, send_sem, bulk_send, bulk_recv, recv_a, recv_b, recv_c,
-    recv_d
+    out_weights, new_o, late_o, unit_v, value_v, decay_v, layer_o,
+    first_heads, pool, one_v, sb, tab, wts, owts, wide, rows_f, every, proj, qkv, units, vals,
+    decs, spread, slots, normed, layer_v,
+    load_sem, tab_sem, w_sem, send_sem, bulk_send, bulk_recv, recv_a, recv_b, recv_c, recv_d,
+    *got
 ):
+    got = list(got) + [late_o]
     me, my_level, member, side_m, twin_m, diag_m, levels = neighbours(count)
     side, twin, diag = (my_level * 4 + m for m in (side_m, twin_m, diag_m))
-    heads, head_size = st.shape[1], st.shape[2]
+    heads, head_size = pool.shape[1], pool.shape[2]
+    st = pool.at[pl.ds(0, row_local)]
     beams = 4 * row_local
     half = member % 2
 
@@ -105,18 +108,18 @@
         sb[slot, :early] = first_heads[chosen[slot]]
     pl.semaphore_wait(barrier, len(peers))
 
-    sent, arriving = [], []
+    sent, arriving, twin_copies = [], [[] for _ in cuts], []
 
     def bulk(index):
         first, length = cuts[index]
         for slot in range(2 * CAP):
             at = index * 2 * CAP + slot
             copy = remote(
-                sb.at[slot, pl.ds(first, length)], got.at[slot, pl.ds(first, length)],
+                sb.at[slot, pl.ds(first, length)], got[index].at[slot],
                 bulk_send.at[at], bulk_recv.at[at], side if slot < CAP else diag,
             )
             copy.start()
-            arriving.append(copy)
+            arriving[index].append(copy)
 
     def send(source, target_ref, sem, target):
         copy = remote(source, target_ref, send_sem.at[len(sent)], sem, target)
@@ -152,9 +155,9 @@
     send(mine, mine, recv_a.at[me], twin)
     state_loads[1].wait()
     for slot in range(2 * CAP):
-        sb[slot, early:] = st[chosen[slot], early:]
+        sb[slot, early:] = pool[chosen[slot], early:]
     for slot in range(2 * CAP, 3 * CAP):
-        sb[slot] = st[chosen[slot]]
+        sb[slot] = pool[chosen[slot]]
     bulk(1)
 
     def took(buffer, sems, block):
@@ -248,12 +251,12 @@
             took(qkv, recv_b, level * 4 + column)
     for slot in range(CAP):
         copy = remote(
-            sb.at[2 * CAP + slot], got_one.at[slot],
+            sb.at[2 * CAP + slot], one_v.at[slot],
             bulk_send.at[len(cuts) * 2 * CAP + slot], bulk_recv.at[len(cuts) * 2 * CAP + slot],
             twin,
         )
         copy.start()
-        arriving.append(copy)
+        twin_copies.append(copy)
 
     for head in range(heads):
         block = qkv[head]
@@ -266,7 +269,7 @@
         spreadq = jnp.concatenate(
             [jnp.where(mask, queries, 0.0).astype(jnp.bfloat16) for mask in masks], axis=1
         )
-        stacked = st[:, head].reshape(row_local * head_size, head_size)
+        stacked = pool[:row_local, head].reshape(row_local * head_size, head_size)
         total = jnp.dot(spreadq, stacked, preferred_element_type=jnp.float32)
         readout = decay * total + jnp.sum(queries * unit, axis=-1, keepdims=True) * values
         scaled = readout * lax.rsqrt(jnp.mean(readout * readout, axis=-1, keepdims=True) + 1e-05)
@@ -282,7 +285,8 @@
 
     forward(slots, recv_c, member, side)
     forward(slots, recv_c, member, twin)
-    bulk(3)
+    for index in range(3, len(cuts)):
+        bulk(index)
     for head in range(heads):
         here = pl.ds(pl.multiple_of(member * row_local, row_local), row_local)
         for target, source in ((unit_v, units), (value_v, vals), (decay_v, decs)):
@@ -301,6 +305,49 @@
         normed[my_level * 2 + core] = level_rows[core * 2 * row_local : (core + 1) * 2 * row_local]
     for other in levels:
         forward(normed, recv_d, my_level * 2 + half, other * 4 + member)
+
+    def collect(index):
+        first, length = cuts[index]
+        for copy in arriving[index]:
+            copy.wait_recv()
+        for slot in range(2 * CAP):
+            pool[row_local + CAP + slot, first : first + length] = got[index][slot]
+
+    def advance(first, last, late):
+        def step(row, carry):
+            base = member * row_local
+            parent = list_s[0, my_level, base + row]
+            block = lax.div(parent, row_local)
+            rank = jnp.int32(0)
+            for earlier in range(row_local):
+                other = lax.div(list_s[0, my_level, base + earlier], row_local)
+                rank = rank + ((other == block) & (earlier < row)).astype(jnp.int32)
+            partner = jnp.bitwise_xor(block, member)
+            rank = jnp.minimum(rank, CAP - 1)
+            source = jnp.where(
+                partner == 0, lax.rem(parent, row_local), row_local + (partner - 1) * CAP + rank
+            )
+            if late:
+                source = jnp.where(partner > 1, 0, source)
+            columns = jnp.transpose(unit_v[row])
+            value, decay = value_v[row], decay_v[row]
+            for head in range(first, last):
+                fresh = columns[:, head : head + 1] * value[head : head + 1, :]
+                prior = pool[source, head].astype(jnp.float32)
+                new_o[row, head] = (decay[head : head + 1, :] * prior + fresh).astype(
+                    jnp.bfloat16
+                )
+            return carry
+
+        lax.fori_loop(0, row_local, step, 0)
+
+    for copy in twin_copies:
+        copy.wait_recv()
+    for slot in range(CAP):
+        pool[row_local + slot] = one_v[slot]
+    for index in range(2):
+        collect(index)
+    advance(0, cuts[2][0], False)
     for other in levels:
         took(normed, recv_d, other * 2 + half)
         forward(normed, recv_d, other * 2 + half, twin)
@@ -318,23 +365,19 @@
                 target = ((level * 2 + line) * 2 + core) * row_local
                 rows = slice(target, target + row_local)
                 layer_v[rows] = rows_f[rows] + attention[source : source + row_local]
-    layer_b[...] = layer_v[...].astype(jnp.bfloat16)
-    outs = [
-        pltpu.make_async_copy(source, target, o_sem.at[k])
-        for k, (source, target) in enumerate(
-            (
-                (unit_v, unit_o), (value_v, value_o), (decay_v, decay_o), (layer_b, layer_o)
-            )
-        )
-    ]
-    for copy in sent:
+    layer_o[...] = layer_v[...].astype(jnp.bfloat16)
+    late = cuts[-1][0]
+    advance(late, heads, True)
+    for index in range(2, len(cuts) - 1):
+        collect(index)
+        advance(cuts[index][0], cuts[index + 1][0], False)
+    for copy in sent + twin_copies:
         copy.wait_send()
-    for copy in outs:
-        copy.start()
-    for copy in arriving:
-        copy.wait()
-    for copy in outs:
-        copy.wait()
+    for copies in arriving:
+        for copy in copies:
+            copy.wait_send()
+    for copy in arriving[-1]:
+        copy.wait_recv()
 
 
 def layer(
@@ -353,22 +396,29 @@
     bf, f32 = jnp.bfloat16, jnp.float32
     dma = pltpu.SemaphoreType.DMA
     rows = (row_local, heads, head_size)
+    whole = states.shape[1:]
+    pool_rows = row_local + 3 * CAP
+
+    def pieces(index):
+        return (2 * CAP, cuts[index][1]) + states.shape[2:]
+
     return pl.pallas_call(
         functools.partial(layer_kernel, count, row_local, tuple(cuts)),
         out_shape=(
-            jax.ShapeDtypeStruct((2 * CAP,) + states.shape[1:], states.dtype),
-            jax.ShapeDtypeStruct((CAP,) + states.shape[1:], states.dtype),
-            jax.ShapeDtypeStruct(rows, f32),
-            jax.ShapeDtypeStruct(rows, f32),
-            jax.ShapeDtypeStruct(rows, f32),
-            jax.ShapeDtypeStruct((row_total, head_size), bf),
+            pltpu.VMEM(states.shape, bf),
+            pltpu.VMEM(pieces(-1), bf),
+            pltpu.VMEM(rows, f32),
+            pltpu.VMEM(rows, f32),
+            pltpu.VMEM(rows, f32),
+            pltpu.VMEM((row_total, head_size), bf),
         ),
         in_specs=[SM, SM, SM, VM, VM, VM, ANY, ANY, ANY, ANY],
-        out_specs=(ANY,) * 6,
+        out_specs=(VM,) * 6,
         scratch_shapes=[
             pltpu.VMEM((row_local, cuts[0][1]) + states.shape[2:], bf),
-            pltpu.VMEM(states.shape, bf),
-            pltpu.VMEM((3 * CAP,) + states.shape[1:], bf),
+            pltpu.VMEM((pool_rows,) + whole, bf),
+            pltpu.VMEM((CAP,) + whole, bf),
+            pltpu.VMEM((3 * CAP,) + whole, bf),
             pltpu.VMEM((table.shape[0] // 8, 8, head_size), bf),
             pltpu.VMEM(weights.shape, bf),
             pltpu.VMEM(out_weight.shape, bf),
@@ -383,15 +433,10 @@
             pltpu.VMEM((beams, heads * head_size), bf),
             pltpu.VMEM((4, slot_count, heads * head_size), bf),
             pltpu.VMEM((count // 2, 2 * row_local, heads * head_size), bf),
-            pltpu.VMEM(rows, f32),
-            pltpu.VMEM(rows, f32),
-            pltpu.VMEM(rows, f32),
             pltpu.VMEM((row_total, head_size), f32),
-            pltpu.VMEM((row_total, head_size), bf),
             dma((2,)),
             dma((4,)),
             dma((2,)),
-            dma((4,)),
             dma((sends,)),
             dma((bulk,)),
             dma((bulk,)),
@@ -399,105 +444,102 @@
             dma((count,)),
             dma((4,)),
             dma((count // 2,)),
-        ],
-        compiler_params=pltpu.CompilerParams(collective_id=1, has_side_effects=True),
+        ]
+        + [pltpu.VMEM(pieces(index), bf) for index in range(len(cuts) - 1)],
+        compiler_params=pltpu.CompilerParams(
+            collective_id=1, has_side_effects=True, vmem_limit_bytes=LAYER_VMEM
+        ),
         name="layer_step",
     )(
-        parents, tokens, gate_bias, parents, gate_weight, norm_gain.reshape(heads, head_size),
-        states, table.reshape(table.shape[0] // 8, 8, head_size), weights, out_weight,
-    )
+        *(
+            pltpu.with_memory_space_constraint(array, pltpu.HBM)
+            for array in (
+                parents, tokens, gate_bias, parents, gate_weight,
+                norm_gain.reshape(heads, head_size), states,
+                table.reshape(table.shape[0] // 8, 8, head_size), weights, out_weight,
+            )
+        ),
+    ), cuts[-1][0]
 
 
 def update_kernel(
-    list_s, states, got, got_one, units, values, decays, layer_in, out_ref, layer_out,
-    old, new, unit_v, value_v, decay_v, layer_v, in_sem, out_sem, side_sem
+    late, list_s, new_in, late_in, units, values, decays, layer_in, out_ref, layer_out, tail,
+    out_sem, side_sem
 ):
-    row_local, heads = old.shape[0], old.shape[1]
+    row_local, heads = new_in.shape[0], new_in.shape[1]
     device = lax.axis_index("rows")
     member, user = device % 4, device // 4
-    sides = [
-        pltpu.make_async_copy(source, target, side_sem.at[k])
-        for k, (source, target) in enumerate(
-            ((units, unit_v), (values, value_v), (decays, decay_v), (layer_in, layer_v))
-        )
+    layer_copy = pltpu.make_async_copy(layer_in, layer_out, side_sem.at[0])
+    layer_copy.start()
+    fronts = [
+        pltpu.make_async_copy(
+            new_in.at[row, pl.ds(0, late)], out_ref.at[row, pl.ds(0, late)],
+            side_sem.at[1 + row],
+        )
+        for row in range(row_local)
     ]
-    for copy in sides:
+    for copy in fronts:
         copy.start()
-    parents = [list_s[0, user, member * row_local + row] for row in range(row_local)]
-    blocks = [lax.div(parent, row_local) for parent in parents]
+    blocks = [
+        lax.div(list_s[0, user, member * row_local + row], row_local) for row in range(row_local)
+    ]
+    span = pl.ds(late, heads - late)
     for row in range(row_local):
         partner = jnp.bitwise_xor(blocks[row], member)
         rank = jnp.int32(0)
         for earlier in range(row):
             rank = rank + (blocks[earlier] == blocks[row]).astype(jnp.int32)
-
-        @pl.when(partner == 0)
+        rank = jnp.minimum(rank, CAP - 1)
+
+        @pl.when(partner < 2)
         def _():
             pltpu.make_async_copy(
-                states.at[lax.rem(parents[row], row_local)], old.at[row], in_sem.at[row]
+                new_in.at[row, span], out_ref.at[row, span], out_sem.at[row]
             ).start()
-
-        @pl.when(partner == 1)
-        def _():
-            pltpu.make_async_copy(got_one.at[rank], old.at[row], in_sem.at[row]).start()
 
         @pl.when(partner > 1)
         def _():
-            pltpu.make_async_copy(
-                got.at[(partner - 2) * CAP + rank], old.at[row], in_sem.at[row]
-            ).start()
-
-    for copy in sides:
+            columns = jnp.transpose(units[row])
+            value, decay = values[row], decays[row]
+            for head in range(late, heads):
+                fresh = columns[:, head : head + 1] * value[head : head + 1, :]
+                prior = late_in[(partner - 2) * CAP + rank, head - late].astype(jnp.float32)
+                tail[row, head - late] = (decay[head : head + 1, :] * prior + fresh).astype(
+                    jnp.bfloat16
+                )
+            pltpu.make_async_copy(tail.at[row], out_ref.at[row, span], out_sem.at[row]).start()
+
+    for row in range(row_local):
+        pltpu.make_async_copy(tail.at[row], out_ref.at[row, span], out_sem.at[row]).wait()
+    for copy in fronts:
         copy.wait()
-    last = pltpu.make_async_copy(layer_v, layer_out, side_sem.at[0])
-    last.start()
-
-    def step(row, carry):
-        pltpu.make_async_copy(states.at[0], old.at[row], in_sem.at[row]).wait()
-        columns = jnp.transpose(unit_v[row])
-        value = value_v[row]
-        decay = decay_v[row]
-        for head in range(heads):
-            fresh = columns[:, head : head + 1] * value[head : head + 1, :]
-            prior = old[row, head].astype(jnp.float32)
-            new[row, head] = (decay[head : head + 1, :] * prior + fresh).astype(jnp.bfloat16)
-        pltpu.make_async_copy(new.at[row], out_ref.at[row], out_sem.at[row]).start()
-        return carry
-
-    lax.fori_loop(0, row_local, step, 0)
-    for row in range(row_local):
-        pltpu.make_async_copy(new.at[row], out_ref.at[row], out_sem.at[row]).wait()
-    last.wait()
-
-
-def update(parents, states, got, got_one, units, values, decays, layer_in):
-    row_local = states.shape[0]
+    layer_copy.wait()
+
+
+def update(late, parents, parts):
+    states, layer_in = parts[0], parts[-1]
+    row_local, heads = states.shape[:2]
     return pl.pallas_call(
-        update_kernel,
+        functools.partial(update_kernel, late),
         out_shape=(
             jax.ShapeDtypeStruct(states.shape, states.dtype),
             jax.ShapeDtypeStruct(layer_in.shape, layer_in.dtype),
         ),
-        in_specs=[SM] + [ANY] * 7,
+        in_specs=[SM] + [VM] * len(parts),
         out_specs=(ANY, ANY),
         scratch_shapes=[
-            pltpu.VMEM(states.shape, states.dtype),
-            pltpu.VMEM(states.shape, states.dtype),
-            pltpu.VMEM(units.shape, units.dtype),
-            pltpu.VMEM(values.shape, values.dtype),
-            pltpu.VMEM(decays.shape, decays.dtype),
-            pltpu.VMEM(layer_in.shape, layer_in.dtype),
+            pltpu.VMEM((row_local, heads - late) + states.shape[2:], states.dtype),
             pltpu.SemaphoreType.DMA((row_local,)),
-            pltpu.SemaphoreType.DMA((row_local,)),
-            pltpu.SemaphoreType.DMA((4,)),
+            pltpu.SemaphoreType.DMA((row_local + 1,)),
         ],
+        compiler_params=pltpu.CompilerParams(vmem_limit_bytes=UPDATE_VMEM),
         cost_estimate=pl.CostEstimate(
-            flops=4 * math.prod(states.shape),
-            bytes_accessed=4 * math.prod(states.shape),
+            flops=math.prod(states.shape),
+            bytes_accessed=2 * math.prod(states.shape),
             transcendentals=0,
         ),
         name="update_states",
-    )(parents, states, got, got_one, units, values, decays, layer_in)
+    )(parents, *(pltpu.with_memory_space_constraint(part, pltpu.VMEM) for part in parts))
 
 
 def fast(
@@ -505,13 +547,11 @@
     out_weight
 ):
     count = lax.axis_size("rows")
-    got, got_one, units, values, decays, layer_mid = layer(
+    parts, late = layer(
         parents, token_ids, gate_bias, gate_weight, norm_gain, states, embed_table,
         jnp.transpose(qkv_weight, (1, 0, 2)), out_weight, count,
     )
-    state_now, layer_out = update(
-        parents, states, got, got_one, units, values, decays, layer_mid
-    )
+    state_now, layer_out = update(late, parents, parts)
     return (layer_out[None], state_now)
 
 

time: 66.2 us -> 61.4 us (0.927)
  Pallas kernels: 64.9 us -> 60.1 us
    pallas_call x1, Pallas kernels: 7.48 us -> 2.73 us  [update(): pl.pallas_call(functools.partial(update_kernel, late), out_shape=(jax.Sha...]
where the time goes in v3:
time: 61.4 us; the launch traced here: 60.8 us
  Pallas kernels  60.1 us (98%)
  between operations  0.66 us (1%)
    pallas_call x1, Pallas kernels, layer(): pl.pallas_call(functools.partial(layer_kernel, count, row_local, tuple(cu...  57.4 us
    pallas_call x1, Pallas kernels, update(): pl.pallas_call(functools.partial(update_kernel, late), out_shape=(jax.Sha...  2.73 us

profile of v3, /device:TPU:0, one launch (start us, length us, event | category | flops | bytes accessed | tf_op | source)
XLA Modules:
  0.0 60.8 jit_solution(2764973048231066946)
XLA Ops:
  0.6 0.0 copy-start
  0.6 57.4 %layer_step.1 = (bf16[8,16,128,128]{3,2,1,0:T(8,128)(2,1)S(1)}, bf16[4,3,128,128]{3,2,1,0:T(8,128)(2,1)S(1)}, f32[8,16,128]{2,1,0:T(8,128)S(1)}, f32[8,16,128]{2...) custom-call(s32[1,4,32]{2,1,0:T(4,128)} %list_s.3, s32[1,128]{1,0:T(1,128)} %tok_s.1, ...), custom_call_target="tpu_custom_call" | custom-call | tf_op jit(solution)/shard_map/layer_step/pallas_call | solution.py:405
  58.0 0.0 copy-done
  58.0 2.7 %update_states.1 = (bf16[8,16,128,128]{3,2,1,0:T(8,128)(2,1)}, bf16[128,128]{1,0:T(8,128)(2,1)}) custom-call(s32[1,4,32]{2,1,0:T(4,128)S(1)} %copy-done, bf16[8,16,128,128]{3,2,1,0:T(8,128)(2,1)S(1)} %get-tuple-element.10.new_in, bf16[4,3,128,128]{3,2,1,0:T(8,128)(2,1)S(1)} %get-tuple-element.11.late_in, f32[8,16,128]{2,1,0:T(8,128)S(1)} %get-tuple-element.12.units, ...), custom_call_target="tpu_custom_call" | custom-call | flops 2097152 | bytes 4194304 | tf_op jit(solution)/shard_map/update_states/pallas_call | solution.py:522
Async XLA Ops:
  0.6 57.4 %copy-start = (s32[1,4,32]{2,1,0:T(4,128)S(1)}, s32[1,4,32]{2,1,0:T(4,128)}, u32[]{:S(2)}) copy-start(s32[1,4,32]{2,1,0:T(4,128)} %list_s.3) | copy-start | bytes 1540
